TPU v7x, 256 devices: a whole 4x4x8 slice. The times are simulated.
256 devices in a mesh: seq: 32 (over y, z), tp: 8 (over x, core).
Axes of the slice: x: 4, y: 4, z: 8, core: 2. Of those that a mesh axis runs over, the one named last changes fastest.
Arguments:
- queries: bfloat16 [16384, 4096], P('seq', 'tp'), may hold values from -36 to 36
- new_keys: bfloat16 [16384, 1024], P('seq', 'tp'), may hold values from -9 to 9
- new_values: bfloat16 [16384, 1024], P('seq', 'tp'), may hold values from -6 to 6
- key_cache: bfloat16 [131072, 1024], P('seq', 'tp'), may hold values from -6 to 6
- value_cache: bfloat16 [131072, 1024], P('seq', 'tp'), may hold values from -6 to 6
- block_lists: int32 [128, 8], P('seq'), may hold values from 0 to 1023, as said below
- out_weight: bfloat16 [4096, 8192], P('tp'), may hold values from -0.09375 to 0.09375
Outputs:
- output: bfloat16 [16384, 8192], P('seq', 'tp')
Inputs may be any that keep to these rules, and one draw needn't show every extreme that they name: For each index of seq, the 32 entries of its rows of block_lists lie at most 4 in the blocks of any one index of seq (blocks s * 32 to (s + 1) * 32 - 1), and some such range holds exactly 4 of them; the entries of one row differ.
All inputs are finite; a program needn't handle non-finite values.
Results may differ from a plain program's by a relative error of at most 0.017.
Values may be sent and summed in bfloat16 or wider, within the bound.
A program may use at most 128 MiB of HBM per device.

v0:
```python
import math

import jax
import jax.numpy as jnp
from jax import lax
from jax.sharding import PartitionSpec as P

HD = 128
BLOCK = 128
TOPB = 8


def body(queries, new_keys, new_values, key_cache, value_cache, block_lists, out_weight):
    seq_count = lax.axis_size("seq")
    my_index = lax.axis_index("seq")
    span_rows, query_width = queries.shape
    cache_rows, kv_width = key_cache.shape
    kv_local = kv_width // HD
    heads_per_kv = query_width // kv_width
    query_blocks = span_rows // BLOCK
    shard_blocks = cache_rows // BLOCK
    slot_count = query_blocks * TOPB
    slot_limit = 4 * ((slot_count + seq_count - 1) // seq_count)
    own_flat = block_lists.reshape(slot_count)
    own_owner = own_flat // shard_blocks
    owner_ids = jnp.arange(seq_count, dtype=jnp.int32)
    matches = (own_owner[None, :] == owner_ids[:, None]).astype(jnp.int32)
    slot_ranking = jnp.cumsum(matches, axis=1) - 1
    own_place = jnp.sum(matches * slot_ranking, axis=0)
    slot_ids = jnp.arange(slot_limit, dtype=jnp.int32)
    every_list = lax.all_gather(block_lists, "seq", axis=0, tiled=True)
    flat_lists = every_list.reshape(seq_count, slot_count)
    owned_here = (flat_lists // shard_blocks == my_index).astype(jnp.int32)
    order_here = jnp.cumsum(owned_here, axis=1) - 1
    selector = owned_here[:, None, :] * (order_here[:, None, :] == slot_ids[None, :, None]).astype(
        jnp.int32
    )
    wanted = jnp.sum(selector * (flat_lists % shard_blocks)[:, None, :], axis=2)
    wanted_flat = wanted.reshape(seq_count * slot_limit)
    key_blocks = key_cache.reshape(shard_blocks, BLOCK, kv_width)
    value_blocks = value_cache.reshape(shard_blocks, BLOCK, kv_width)
    sent_keys = key_blocks[wanted_flat].reshape(seq_count, slot_limit, BLOCK, kv_width)
    sent_values = value_blocks[wanted_flat].reshape(seq_count, slot_limit, BLOCK, kv_width)
    got_keys, got_values = (
        lax.all_to_all(sent_keys, "seq", split_axis=0, concat_axis=0, tiled=True),
        lax.all_to_all(sent_values, "seq", split_axis=0, concat_axis=0, tiled=True),
    )
    where_from = own_owner * slot_limit + own_place
    listed_rows = TOPB * BLOCK
    listed_keys = got_keys.reshape(seq_count * slot_limit, BLOCK, kv_width)[where_from].reshape(
        query_blocks, listed_rows, kv_local, HD
    )
    listed_values = got_values.reshape(seq_count * slot_limit, BLOCK, kv_width)[where_from].reshape(
        query_blocks, listed_rows, kv_local, HD
    )
    query_tiles = queries.reshape(query_blocks, BLOCK, kv_local, heads_per_kv, HD)
    fresh_keys = new_keys.reshape(query_blocks, BLOCK, kv_local, HD)
    fresh_values = new_values.reshape(query_blocks, BLOCK, kv_local, HD)
    score_scale = 1.0 / math.sqrt(HD)
    row_ids = jnp.arange(BLOCK, dtype=jnp.int32)[:, None]
    col_ids = jnp.arange(listed_rows + BLOCK, dtype=jnp.int32)[None, :]
    visible = (col_ids < listed_rows) | (col_ids - listed_rows <= row_ids)

    def attend(pieces):
        query_tile, far_keys, far_values, own_keys, own_values = pieces
        all_keys = jnp.concatenate([far_keys, own_keys], axis=0)
        all_values = jnp.concatenate([far_values, own_values], axis=0)
        scores = (
            jnp.einsum("ikgd,jkd->kgij", query_tile, all_keys, preferred_element_type=jnp.float32)
            * score_scale
        )
        scores = jnp.where(visible[None, None], scores, -1e30)
        largest = jnp.max(scores, axis=-1, keepdims=True)
        expanded = jnp.exp(scores - largest)
        weights = (expanded / jnp.sum(expanded, axis=-1, keepdims=True)).astype(jnp.bfloat16)
        mixed = jnp.einsum(
            "kgij,jkd->ikgd", weights, all_values, preferred_element_type=jnp.float32
        )
        return mixed.astype(jnp.bfloat16).reshape(BLOCK, query_width)

    attended = lax.map(
        attend, (query_tiles, listed_keys, listed_values, fresh_keys, fresh_values)
    ).reshape(span_rows, query_width)
    partial_term = jnp.dot(attended, out_weight, preferred_element_type=jnp.float32)
    summed = lax.psum_scatter(
        partial_term.astype(jnp.bfloat16), "tp", scatter_dimension=1, tiled=True
    )
    return summed


def solution(mesh):
    in_specs = (
        P("seq", "tp"),
        P("seq", "tp"),
        P("seq", "tp"),
        P("seq", "tp"),
        P("seq", "tp"),
        P("seq", None),
        P("tp", None),
    )
    out_specs = P("seq", "tp")
    return jax.shard_map(body, mesh=mesh, in_specs=in_specs, out_specs=out_specs, check_vma=False)
```

profile of v0, /device:TPU:1, one launch (start us, length us, event | category | flops | bytes accessed | tf_op | source)
XLA Modules:
  0.0 366.2 jit_solution(402416970448712453)
XLA Ops:
  6.5 40.7 %all-gather = s32[32,4,8]{2,1,0:T(4,128)S(1)} all-gather(s32[1,4,8]{2,1,0:T(4,128)} %bitcast.88), channel_id=1, replica_groups=mesh['seq'=32,'tp'=8] {'seq'}, dimensions={0}, use_global_device_ids=true | all-gather | bytes 4224 | tf_op jit(solution)/shard_map/all_gather | solution.py:31
  48.0 3.1 gather_fusion.2
  51.0 6.1 %all-to-all-start.1 = ((bf16[32,4,128,128]{3,2,1,0:T(8,128)(2,1)}), bf16[32,4,128,128]{3,2,1,0:T(8,128)(2,1)}, u32[]{:S(2)}, u32[]{:S(2)}) async-start(bf16[32,4,128,128]{3,2,1,0:T(8,128)(2,1)} %bitcast.80), calls=%async_computation.1 | async-start | bytes 8388608 | tf_op jit(solution)/shard_map/all_to_all | solution.py:45
  57.2 3.1 gather_fusion
  60.2 79.3 %all-to-all-done.1 = bf16[32,4,128,128]{3,2,1,0:T(8,128)(2,1)} async-done(((bf16[32,4,128,128]{3,2,1,0:T(8,128)(2,1)}), bf16[32,4,128,128]{3,2,1,0:T(8,128)(2,1)}, u32[]{:S(2)}, u32[]{:S(2)}) %all-to-all-start.1) | async-done | bytes 4194336 | tf_op jit(solution)/shard_map/all_to_all | solution.py:45
  139.6 7.8 %all-to-all-start = ((bf16[32,4,128,128]{3,2,1,0:T(8,128)(2,1)}), bf16[32,4,128,128]{3,2,1,0:T(8,128)(2,1)}, u32[]{:S(2)}, u32[]{:S(2)}) async-start(bf16[32,4,128,128]{3,2,1,0:T(8,128)(2,1)} %bitcast.79), calls=%async_computation | async-start | bytes 8388608 | tf_op jit(solution)/shard_map/all_to_all | solution.py:46
  148.9 3.9 %gather_fusion.3 = bf16[32,128,128]{2,1,0:T(8,128)(2,1)} fusion(bf16[128,128,128]{2,1,0:T(8,128)(2,1)} %bitcast.12, s32[1024]{0:T(1024)S(1)} %pad_clamp_fusion), kind=kCustom, calls=%fused_computation.3 | custom fusion | bytes 2097280 | tf_op jit(solution)/shard_map/gather | solution.py:50
  152.8 78.9 %all-to-all-done = bf16[32,4,128,128]{3,2,1,0:T(8,128)(2,1)} async-done(((bf16[32,4,128,128]{3,2,1,0:T(8,128)(2,1)}), bf16[32,4,128,128]{3,2,1,0:T(8,128)(2,1)}, u32[]{:S(2)}, u32[]{:S(2)}) %all-to-all-start) | async-done | bytes 4194336 | tf_op jit(solution)/shard_map/all_to_all | solution.py:46
  231.7 3.8 %gather_fusion.1 = bf16[32,128,128]{2,1,0:T(8,128)(2,1)} fusion(bf16[128,128,128]{2,1,0:T(8,128)(2,1)} %bitcast.5, s32[1024]{0:T(1024)S(1)} %pad_clamp_fusion), kind=kCustom, calls=%fused_computation.1 | custom fusion | bytes 2097280 | tf_op jit(solution)/shard_map/gather | solution.py:53
  235.5 48.7 %while.11 = (s32[]{:T(128)}, bf16[4,128,512]{2,1,0:T(8,128)(2,1)}, bf16[4,1024,1,128]{3,1,0,2:T(8,128)(2,1)}, bf16[4,128,1,128]{3,1,0,2:T(8,128)(2,1)}, bf16[4,1...) while((s32[]{:T(128)}, bf16[4,128,512]{2,1,0:T(8,128)(2,1)}, ...), condition=%wide.region_7.8_spmd.clone, body=%wide.region_4.7_spmd.clone.sunk | while | flops 308247552 | bytes 10797305 | solution.py:81
  235.5 1.0 dynamic-slice_bitcast_fusion.5
  236.5 1.0 constant_dynamic-slice_fusion.6
  240.5 1.7 constant_dynamic-slice_fusion.8
  242.1 1.8 copy.56
  245.4 1.5 fusion.36
  247.7 1.0 dynamic-slice_bitcast_fusion.5
  248.7 1.0 constant_dynamic-slice_fusion.6
  252.7 1.7 constant_dynamic-slice_fusion.8
  254.3 1.8 copy.56
  257.6 1.5 fusion.36
  259.9 1.0 dynamic-slice_bitcast_fusion.5
  260.9 1.0 constant_dynamic-slice_fusion.6
  264.9 1.7 constant_dynamic-slice_fusion.8
  266.5 1.8 copy.56
  269.8 1.5 fusion.36
  272.1 1.0 dynamic-slice_bitcast_fusion.5
  273.0 1.0 constant_dynamic-slice_fusion.6
  277.0 1.7 constant_dynamic-slice_fusion.8
  278.7 1.8 copy.56
  281.9 1.5 fusion.36
  284.3 11.3 %convolution_convert_fusion = bf16[512,8192]{1,0:T(8,128)(2,1)} fusion(bf16[512,512]{1,0:T(8,128)(2,1)} %bitcast.89, bf16[512,8192]{1,0:T(8,128)(2,1)} %param.15), kind=kOutput, calls=%fused_computation.31 | convolution fusion | flops 4299161600 | bytes 17301504 | tf_op jit(solution)/shard_map/dot_general | solution.py:84
  295.6 63.7 %reduce-scatter.2.cloned.1.call-done = bf16[512,1024]{1,0:T(8,128)(2,1)} async-done(((bf16[512,8192]{1,0:T(8,128)(2,1)}), bf16[512,1024]{1,0:T(8,128)(2,1)}) %reduce-scatter.2.cloned.1.call-update) | async-done | bytes 1048592 | tf_op jit(solution)/shard_map/reduce_scatter | solution.py:85
  (64 shorter events, 23.2 us)
Async XLA Ops:
  6.5 41.4 %copy-start = (bf16[4096,128]{1,0:T(8,128)(2,1)S(1)}, bf16[4096,128]{1,0:T(8,128)(2,1)}, u32[]{:S(2)}) copy-start(bf16[4096,128]{1,0:T(8,128)(2,1)} %param.12) | copy-start | bytes 3145732
  51.0 6.1 %copy-start.1 = (bf16[4096,128]{1,0:T(8,128)(2,1)S(1)}, bf16[4096,128]{1,0:T(8,128)(2,1)}, u32[]{:S(2)}) copy-start(bf16[4096,128]{1,0:T(8,128)(2,1)} %param.13) | copy-start | bytes 3145732
  51.0 88.5 %all-to-all-start.1 = ((bf16[32,4,128,128]{3,2,1,0:T(8,128)(2,1)}), bf16[32,4,128,128]{3,2,1,0:T(8,128)(2,1)}, u32[]{:S(2)}, u32[]{:S(2)}) async-start(bf16[32,4,128,128]{3,2,1,0:T(8,128)(2,1)} %bitcast.80), calls=%async_computation.1 | async-start | bytes 8388608 | tf_op jit(solution)/shard_map/all_to_all | solution.py:45
  139.6 7.9 %copy-start.3 = (s32[4,8]{1,0:T(4,128)S(1)}, s32[4,8]{1,0:T(4,128)}, u32[]{:S(2)}) copy-start(s32[4,8]{1,0:T(4,128)} %param.14) | copy-start | bytes 388
  139.6 8.3 %copy-start.2 = (bf16[512,512]{1,0:T(8,128)(2,1)S(1)}, bf16[512,512]{1,0:T(8,128)(2,1)}, u32[]{:S(2)}) copy-start(bf16[512,512]{1,0:T(8,128)(2,1)} %param.9) | copy-start | bytes 1572868
  139.6 92.1 %all-to-all-start = ((bf16[32,4,128,128]{3,2,1,0:T(8,128)(2,1)}), bf16[32,4,128,128]{3,2,1,0:T(8,128)(2,1)}, u32[]{:S(2)}, u32[]{:S(2)}) async-start(bf16[32,4,128,128]{3,2,1,0:T(8,128)(2,1)} %bitcast.79), calls=%async_computation | async-start | bytes 8388608 | tf_op jit(solution)/shard_map/all_to_all | solution.py:46
  147.4 211.9 %reduce-scatter.2.cloned.1.call-start = ((), (), s32[]{:S(2)}) async-start(), calls=%async_computation.3 | async-start | bytes 9437184 | tf_op jit(solution)/shard_map/reduce_scatter | solution.py:85
Sparse Core Ops, SparseCore 0:
  295.7 63.5 reduce-scatter.1
where the time goes:
time: 368 us; the launch traced here: 366 us
  waiting for transfers between devices  222 us (60%)
  local copies, waits for them, and re-layouts  48.8 us (13%)
  blocking collectives  40.7 us (11%)
  matrix products  19.3 us (5%)
  starting transfers between devices  14 us (4%)
  between operations  13.5 us (4%)
  other arithmetic  7.74 us (2%)
    all_to_all x1, waiting for transfers between devices, body(): lax.all_to_all(sent_keys, 'seq', split_axis=0, concat_axis=0, tiled=True)  79.3 us
    all_to_all x1, waiting for transfers between devices, body(): lax.all_to_all(sent_values, 'seq', split_axis=0, concat_axis=0, tiled=True)  78.9 us
    reduce_scatter x1, waiting for transfers between devices, body(): lax.psum_scatter(partial_term.astype(jnp.bfloat16), 'tp', scatter_dimensi...  63.7 us
    all_gather x1, blocking collectives, body(): every_list = lax.all_gather(block_lists, 'seq', axis=0, tiled=True)  40.7 us
    dynamic_slice x20, local copies, waits for them, and re-layouts, body(): lax.map(attend, (query_tiles, listed_keys, listed_values, fresh_keys, fre...  23.5 us
    dot_general x1, matrix products, body(): jnp.dot(attended, out_weight, preferred_element_type=jnp.float32)  11.3 us
    all_to_all x1, starting transfers between devices, body(): lax.all_to_all(sent_values, 'seq', split_axis=0, concat_axis=0, tiled=True)  7.85 us
  transfers between devices with their start and end apart: 3, of which 3 were waited for; matrix products, arithmetic and copies ran while one was open for 2% of the time, Pallas kernels for 0%

commit v1 on v0

v1 whole, which is shorter than its diff:
```python
import functools
import math

import jax
import jax.numpy as jnp
from jax import lax
from jax.experimental import pallas as pl
from jax.experimental.pallas import tpu as pltpu
from jax.sharding import PartitionSpec as P

HD = 128
BLOCK = 128
TOPB = 8
NY, NZ, NX, NC = 4, 8, 4, 2
SEQ = NY * NZ
TP = NX * NC
SHARD = 32
QBD = 4
ENT = QBD * TOPB
G = 4
CAPS = (8, 24, 32, 32)
PARTS = 2
ROWS = BLOCK // PARTS
CHUNKS = 2 * PARTS
MESH = pl.DeviceIdType.MESH
F32 = jnp.float32
BF16 = jnp.bfloat16


def lists_kernel(own_ref, out_ref, send_sem, recv_sem):
    me = lax.axis_index("seq")
    barrier = pltpu.get_barrier_semaphore()

    def greet(i, carry):
        peer = lax.rem(me + i, SEQ)
        pl.semaphore_signal(barrier, inc=1, device_id={"seq": peer}, device_id_type=MESH)
        return carry

    lax.fori_loop(1, SEQ, greet, 0)
    pl.semaphore_wait(barrier, SEQ - 1)

    def copy(i):
        peer = lax.rem(me + i, SEQ)
        return pltpu.make_async_remote_copy(
            src_ref=own_ref,
            dst_ref=out_ref.at[me],
            send_sem=send_sem.at[i],
            recv_sem=recv_sem.at[i],
            device_id={"seq": peer},
            device_id_type=MESH,
        )

    def start(i, carry):
        copy(i).start()
        return carry

    lax.fori_loop(1, SEQ, start, 0)
    out_ref[me] = own_ref[...]

    def finish(i, carry):
        copy(i).wait()
        return carry

    lax.fori_loop(1, SEQ, finish, 0)


def gather_lists(block_lists):
    padded = jnp.pad(block_lists.reshape(1, ENT), ((0, 7), (0, 128 - ENT)))
    every = pl.pallas_call(
        lists_kernel,
        out_shape=jax.ShapeDtypeStruct((SEQ, 8, 128), jnp.int32),
        in_specs=[pl.BlockSpec(memory_space=pltpu.VMEM)],
        out_specs=pl.BlockSpec(memory_space=pltpu.VMEM),
        scratch_shapes=[
            pltpu.SemaphoreType.DMA((SEQ,)),
            pltpu.SemaphoreType.DMA((SEQ,)),
        ],
        compiler_params=pltpu.CompilerParams(collective_id=0, has_side_effects=True),
        name="gather_lists",
    )(padded)
    return every[:, 0, :ENT]


def route_tables(every):
    me = lax.axis_index("seq")
    y, z = me // NZ, me % NZ
    row = lax.dynamic_slice_in_dim(every, y * NZ, NZ, axis=0)
    rel = lax.dynamic_slice_in_dim(jnp.concatenate([row, row], axis=0), z, NZ, axis=0)
    k = jnp.arange(NZ, dtype=jnp.int32)[:, None]
    owner = rel // SHARD
    spot = (owner // NZ) * SHARD + rel % SHARD
    du = (z + k - owner % NZ + NZ) % NZ
    e = jnp.arange(ENT, dtype=jnp.int32)
    before = (e[None, :] < e[:, None])[None]
    half = du == NZ // 2
    rank = jnp.sum((before & half[:, None, :]).astype(jnp.int32), axis=2)
    up = ((du >= 1) & (du <= 3)) | (half & (rank % 2 == 0))
    down = (du >= 5) | (half & (rank % 2 == 1))
    way = up.astype(jnp.int32) + 2 * down.astype(jnp.int32)
    dist = jnp.where(down, NZ - du, du)
    order = (NZ - dist) * ENT + e[None, :]
    ahead = (way[:, None, :] == way[:, :, None]) & (order[:, None, :] < order[:, :, None])
    place = jnp.sum(ahead.astype(jnp.int32), axis=2)
    k_up = jnp.array([4, 3, 2, 1], jnp.int32)
    rel_up = jnp.stack([rel_row for rel_row in (4, 3, 2, 1)]) if False else k_up
    take = lambda a: jnp.concatenate([a[4:5], a[3:4], a[2:3], a[1:2], a[4:5], a[5:6], a[6:7], a[7:8]])
    want_way = jnp.array([1, 1, 1, 1, 2, 2, 2, 2], jnp.int32)[:, None]
    want_dist = jnp.concatenate([rel_up, k_up])[:, None]
    mine = (take(way) == want_way) & (take(dist) == want_dist)
    hit = mine[:, None, :] & (take(place)[:, None, :] == e[None, :, None])
    steps = jnp.sum(hit.astype(jnp.int32) * (take(spot)[:, None, :] + 1), axis=2) - 1
    last = jnp.stack(
        [
            way[0],
            jnp.where(way[0] == 1, place[0], 0),
            jnp.where(way[0] == 2, place[0], 0),
            jnp.where(way[0] == 0, spot[0], 0),
        ]
    )
    return jnp.concatenate([steps, last], axis=0)


def main_kernel(
    tab,
    q_hbm,
    nk_hbm,
    nv_hbm,
    kc_hbm,
    vc_hbm,
    w_hbm,
    out_ref,
    cols,
    hops,
    fins,
    kg,
    vg,
    q,
    probs,
    att,
    w_all,
    w_relay,
    y_send,
    y_recv,
    z_send,
    z_recv,
    w_send,
    w_recv,
    a_send,
    a_recv,
    local_sem,
):
    s = lax.axis_index("seq")
    t = lax.axis_index("tp")
    y, z = s // NZ, lax.rem(s, NZ)
    x, c = t // NC, lax.rem(t, NC)
    yp = lax.rem(y + 1, NY) * NZ + z
    ym = lax.rem(y + NY - 1, NY) * NZ + z
    zp = y * NZ + lax.rem(z + 1, NZ)
    zm = y * NZ + lax.rem(z + NZ - 1, NZ)
    xp = lax.rem(x + 1, NX)
    xm = lax.rem(x + NX - 1, NX)
    xo = lax.rem(x + 2, NX)
    sib = x * NC + (1 - c)

    def remote(src, dst, ssem, rsem, seq=None, tp=None):
        return pltpu.make_async_remote_copy(
            src_ref=src,
            dst_ref=dst,
            send_sem=ssem,
            recv_sem=rsem,
            device_id={"seq": s if seq is None else seq, "tp": t if tp is None else tp},
            device_id_type=MESH,
        )

    barrier = pltpu.get_barrier_semaphore()
    peers = [(yp, t), (ym, t), (zp, t), (zm, t), (s, sib)]
    peers += [(s, xx * NC + cc) for xx in (xp, xm) for cc in range(NC)]
    for ps, pt in peers:
        pl.semaphore_signal(
            barrier, inc=1, device_id={"seq": ps, "tp": pt}, device_id_type=MESH
        )

    pending = []

    locals_ = []

    def local(src, dst):
        cp = pltpu.make_async_copy(src, dst, local_sem.at[len(locals_)])
        cp.start()
        locals_.append(cp)
        return cp

    def source(ch):
        ref = kc_hbm if ch < PARTS else vc_hbm
        return ref.at[:, pl.ds((ch % PARTS) * ROWS, ROWS), :]

    own_rows = pl.ds(pl.multiple_of(y * SHARD, SHARD), SHARD)
    own_cols = [local(source(ch), cols[ch].at[own_rows]) for ch in range(CHUNKS)]
    in_q = local(q_hbm, q)
    in_nk = [local(nk_hbm.at[pl.ds(b * BLOCK, BLOCK)], kg.at[b, pl.ds(TOPB * BLOCK, BLOCK)]) for b in range(QBD)]
    in_nv = [local(nv_hbm.at[pl.ds(b * BLOCK, BLOCK)], vg.at[b, pl.ds(TOPB * BLOCK, BLOCK)]) for b in range(QBD)]

    pl.semaphore_wait(barrier, len(peers))

    half = SHARD // 2
    y_copies = []

    def y_start(ch):
        mine = [
            remote(source(ch), cols[ch].at[own_rows], y_send.at[ch, 0], y_recv.at[ch, 0], seq=yp),
            remote(source(ch), cols[ch].at[own_rows], y_send.at[ch, 1], y_recv.at[ch, 1], seq=ym),
        ]
        for cp in mine:
            cp.start()
        y_copies.append(mine)
        pending.extend(mine)

    def y_relay(ch):
        first, second = y_copies[ch]
        first.wait_recv()
        lo = pl.ds(pl.multiple_of(lax.rem(y + NY - 1, NY) * SHARD, SHARD), half)
        a = remote(cols[ch].at[lo], cols[ch].at[lo], y_send.at[ch, 2], y_recv.at[ch, 2], seq=yp)
        a.start()
        second.wait_recv()
        hi = pl.ds(pl.multiple_of(lax.rem(y + 1, NY) * SHARD + half, half), half)
        b = remote(cols[ch].at[hi], cols[ch].at[hi], y_send.at[ch, 3], y_recv.at[ch, 3], seq=ym)
        b.start()
        pending.extend([a, b])
        return a, b

    z_copies = {}
    seg = 4

    def merge(ch, d, step):
        cap = CAPS[step]
        kept = CAPS[step - 1] if step else 0
        buf = hops[d][step][ch]

        def fresh(j):
            at = tab[d * 4 + step, j]
            return at, cols[ch][jnp.maximum(at, 0)]

        def both(i, carry):
            for u in range(seg):
                j = i * seg + u
                at, new = fresh(j)
                buf[j] = jnp.where(at < 0, buf[j], new)
            return carry

        def only(i, carry):
            for u in range(seg):
                j = i * seg + u
                buf[j] = fresh(j)[1]
            return carry

        if kept:
            lax.fori_loop(0, kept // seg, both, 0)
        if cap > kept:
            lax.fori_loop(kept // seg, cap // seg, only, 0)

    def z_step(ch, step):
        for d in range(2):
            if step:
                z_copies[ch, d, step - 1].wait_recv()
            merge(ch, d, step)
            if step < 3:
                dst = hops[d][step + 1][ch].at[pl.ds(0, CAPS[step])]
            else:
                dst = fins[d][ch]
            cp = remote(
                hops[d][step][ch],
                dst,
                z_send.at[ch, d, step],
                z_recv.at[ch, d, step],
                seq=zp if d == 0 else zm,
            )
            cp.start()
            z_copies[ch, d, step] = cp
            pending.append(cp)

    def collect(ch):
        for d in range(2):
            z_copies[ch, d, 3].wait_recv()
        dst = kg if ch < PARTS else vg
        r0 = (ch % PARTS) * ROWS
        for b in range(QBD):

            def entry(i, carry):
                e = b * TOPB + i
                way = tab[8, e]
                val = jnp.where(
                    way == 0,
                    cols[ch][tab[11, e]],
                    jnp.where(way == 1, fins[0][ch][tab[9, e]], fins[1][ch][tab[10, e]]),
                )
                dst[b, pl.ds(pl.multiple_of(i * BLOCK + r0, ROWS), ROWS), :] = val
                return carry

            lax.fori_loop(0, TOPB, entry, 0)

    depth = G * HD
    width = w_hbm.shape[1] // TP
    hd = depth // 2

    def w_cols(tt):
        return pl.ds(pl.multiple_of(tt * width, width), width)

    def w_rows(tt, off=0, n=depth):
        return pl.ds(pl.multiple_of(tt * depth + off, hd), n)

    w_direct, w_first = [], []

    def w_start():
        targets = [sib] + [xx * NC + cc for xx in (xp, xm) for cc in range(NC)]
        slots = [0, 1 + c, 1 + c, 3 + c, 3 + c]
        for dirn in range(2):
            for cc in range(NC):
                cp = remote(
                    w_hbm.at[pl.ds(dirn * hd, hd), w_cols(xo * NC + cc)],
                    w_relay.at[dirn * NC + cc],
                    w_send.at[5 + dirn * NC + cc],
                    w_recv.at[5 + dirn * NC + cc],
                    tp=(xp if dirn == 0 else xm) * NC + c,
                )
                cp.start()
                w_first.append(cp)
                pending.append(cp)
        for i, (tt, slot) in enumerate(zip(targets, slots)):
            cp = remote(
                w_hbm.at[:, w_cols(tt)],
                w_all.at[w_rows(t)],
                w_send.at[i],
                w_recv.at[slot],
                tp=tt,
            )
            cp.start()
            w_direct.append(cp)
            pending.append(cp)

    w_second = []

    def w_forward():
        for dirn in range(2):
            for cc in range(NC):
                w_first[dirn * NC + cc].wait_recv()
                src_t = (xm if dirn == 0 else xp) * NC + c
                dst_t = (xp if dirn == 0 else xm) * NC + cc
                rows = w_rows(src_t, dirn * hd, hd)
                cp = remote(
                    w_relay.at[dirn * NC + cc],
                    w_all.at[rows],
                    w_send.at[9 + dirn * NC + cc],
                    w_recv.at[9 + dirn * NC + c],
                    tp=dst_t,
                )
                cp.start()
                w_second.append(cp)
                pending.append(cp)

    def w_wait():
        for slot in range(5):
            remote(
                w_hbm.at[:, w_cols(t)], w_all.at[w_rows(t)], w_send.at[0], w_recv.at[slot], tp=sib
            ).wait_recv()
        for slot in range(4):
            remote(
                w_relay.at[slot],
                w_all.at[w_rows(t, 0, hd)],
                w_send.at[9],
                w_recv.at[9 + slot],
                tp=sib,
            ).wait_recv()

    y_start(0)
    w_own = local(w_hbm.at[:, w_cols(t)], w_all.at[w_rows(t)])
    w_start()

    relays = {}

    def y_finish(ch):
        own_cols[ch].wait()
        relays[ch] = y_relay(ch)
        if ch + 1 < CHUNKS:
            y_start(ch + 1)
        for cp in relays[ch]:
            cp.wait_recv()

    def scores(b):
        rows = pl.ds(pl.multiple_of(b * BLOCK, BLOCK), BLOCK)
        keys = kg[b]
        seen = TOPB * BLOCK
        row_ids = lax.broadcasted_iota(jnp.int32, (BLOCK, BLOCK), 0)
        col_ids = lax.broadcasted_iota(jnp.int32, (BLOCK, BLOCK), 1)
        for g in range(G):
            qt = q[rows, g * HD : (g + 1) * HD]
            sc = lax.dot_general(
                qt, keys, (((1,), (1,)), ((), ())), preferred_element_type=F32
            ) * (1.0 / math.sqrt(HD))
            near = jnp.where(col_ids <= row_ids, sc[:, seen:], -1e30)
            far = sc[:, :seen]
            top = jnp.maximum(
                jnp.max(far, axis=1, keepdims=True), jnp.max(near, axis=1, keepdims=True)
            )
            ef = jnp.exp(far - top)
            en = jnp.exp(near - top)
            tot = jnp.sum(ef, axis=1, keepdims=True) + jnp.sum(en, axis=1, keepdims=True)
            inv = 1.0 / tot
            probs[b, g * BLOCK : (g + 1) * BLOCK, :seen] = (ef * inv).astype(BF16)
            probs[b, g * BLOCK : (g + 1) * BLOCK, seen:] = (en * inv).astype(BF16)

    def mix(b):
        o = jnp.dot(probs[b], vg[b], preferred_element_type=F32).astype(BF16)
        for g in range(G):
            att[t, b, :, g * HD : (g + 1) * HD] = o[g * BLOCK : (g + 1) * BLOCK]

    forwarded = False
    for wave in range(CHUNKS + 4):
        for ch in range(CHUNKS):
            step = wave - ch
            if step < 0 or step > 4:
                continue
            if step == 0:
                y_finish(ch)
            if step < 4:
                z_step(ch, step)
            else:
                collect(ch)
                if ch == PARTS - 1:
                    in_q.wait()
                    for cp in in_nk:
                        cp.wait()

                    def score_step(b, carry):
                        scores(b)
                        return carry

                    lax.fori_loop(0, QBD, score_step, 0)
        if wave == 3:
            w_forward()

    for cp in in_nv:
        cp.wait()

    hb = BLOCK // 2
    a_first, a_second, a_third = {}, {}, {}

    def sem(b, i):
        return a_send.at[b, i], a_recv.at[b, i]

    def stage_a(b):
        mix(b)
        cps = [
            remote(att.at[t, b], att.at[t, b], *sem(b, i), tp=tt)
            for i, tt in enumerate((xp * NC + c, xm * NC + c, sib))
        ]
        for cp in cps:
            cp.start()
        a_first[b] = cps
        pending.extend(cps)

    lo, hi = pl.ds(0, hb), pl.ds(hb, hb)

    def stage_b(b):
        tm, tpl = xm * NC + c, xp * NC + c
        a_first[b][0].wait_recv()
        cps = [
            remote(att.at[tm, b, lo], att.at[tm, b, lo], *sem(b, 3), tp=tpl),
            remote(att.at[tm, b], att.at[tm, b], *sem(b, 4), tp=sib),
        ]
        for cp in cps:
            cp.start()
        a_first[b][1].wait_recv()
        more = [
            remote(att.at[tpl, b, hi], att.at[tpl, b, hi], *sem(b, 5), tp=tm),
            remote(att.at[tpl, b], att.at[tpl, b], *sem(b, 6), tp=sib),
        ]
        for cp in more:
            cp.start()
        a_second[b] = cps + more
        pending.extend(a_second[b])

    def stage_c(b):
        to = xo * NC + c
        a_second[b][0].wait_recv()
        a_second[b][2].wait_recv()
        cp = remote(att.at[to, b], att.at[to, b], *sem(b, 7), tp=sib)
        cp.start()
        a_third[b] = cp
        pending.append(cp)

    def stage_d(b):
        a_first[b][2].wait_recv()
        a_second[b][1].wait_recv()
        a_second[b][3].wait_recv()
        a_third[b].wait_recv()
        acc = jnp.zeros((BLOCK, width), F32)
        for tt in range(TP):
            acc += jnp.dot(
                att[tt, b], w_all[tt * depth : (tt + 1) * depth, :], preferred_element_type=F32
            )
        out_ref[b * BLOCK : (b + 1) * BLOCK, :] = acc.astype(BF16)

    for b in range(QBD):
        stage_a(b)
    w_own.wait()
    w_wait()
    stage_b(0)
    stage_b(1)
    stage_c(0)
    stage_b(2)
    stage_c(1)
    stage_d(0)
    stage_b(3)
    stage_c(2)
    stage_d(1)
    stage_c(3)
    stage_d(2)
    stage_d(3)

    for cp in pending:
        cp.wait_send()


def exchange(table, queries, new_keys, new_values, key_cache, value_cache, out_weight):
    any_ = pl.BlockSpec(memory_space=pl.ANY)
    width = out_weight.shape[1] // TP
    blk = lambda n: pltpu.VMEM((n, ROWS, HD), BF16)
    hop_bufs = [[[blk(CAPS[i]) for _ in range(CHUNKS)] for i in range(4)] for _ in range(2)]
    fin_bufs = [[blk(CAPS[3]) for _ in range(CHUNKS)] for _ in range(2)]
    scratch = [
        [blk(NY * SHARD) for _ in range(CHUNKS)],
        hop_bufs,
        fin_bufs,
        pltpu.VMEM((QBD, (TOPB + 1) * BLOCK, HD), BF16),
        pltpu.VMEM((QBD, (TOPB + 1) * BLOCK, HD), BF16),
        pltpu.VMEM((QBD * BLOCK, G * HD), BF16),
        pltpu.VMEM((QBD, G * BLOCK, (TOPB + 1) * BLOCK), BF16),
        pltpu.VMEM((TP, QBD, BLOCK, G * HD), BF16),
        pltpu.VMEM((TP * G * HD, width), BF16),
        pltpu.VMEM((4, G * HD // 2, width), BF16),
        pltpu.SemaphoreType.DMA((CHUNKS, 4)),
        pltpu.SemaphoreType.DMA((CHUNKS, 4)),
        pltpu.SemaphoreType.DMA((CHUNKS, 2, 4)),
        pltpu.SemaphoreType.DMA((CHUNKS, 2, 4)),
        pltpu.SemaphoreType.DMA((13,)),
        pltpu.SemaphoreType.DMA((13,)),
        pltpu.SemaphoreType.DMA((QBD, 8)),
        pltpu.SemaphoreType.DMA((QBD, 8)),
        pltpu.SemaphoreType.DMA((CHUNKS + 2 + 2 * QBD,)),
    ]
    flat, tree = jax.tree.flatten(scratch)
    fixed = 8

    def kernel(*refs):
        main_kernel(*refs[:fixed], *jax.tree.unflatten(tree, refs[fixed:]))

    return pl.pallas_call(
        kernel,
        out_shape=jax.ShapeDtypeStruct((QBD * BLOCK, width), BF16),
        in_specs=[pl.BlockSpec(memory_space=pltpu.SMEM)] + [any_] * 6,
        out_specs=pl.BlockSpec(memory_space=pltpu.VMEM),
        scratch_shapes=flat,
        compiler_params=pltpu.CompilerParams(
            collective_id=1, has_side_effects=True, vmem_limit_bytes=60 * 1024 * 1024
        ),
        name="exchange",
    )(
        table,
        queries,
        new_keys,
        new_values,
        key_cache.reshape(SHARD, BLOCK, HD),
        value_cache.reshape(SHARD, BLOCK, HD),
        out_weight,
    )


def body(queries, new_keys, new_values, key_cache, value_cache, block_lists, out_weight):
    every = gather_lists(block_lists)
    table = route_tables(every)
    return exchange(table, queries, new_keys, new_values, key_cache, value_cache, out_weight)


def solution(mesh):
    in_specs = (
        P("seq", "tp"),
        P("seq", "tp"),
        P("seq", "tp"),
        P("seq", "tp"),
        P("seq", "tp"),
        P("seq", None),
        P("tp", None),
    )
    out_specs = P("seq", "tp")
    return jax.shard_map(body, mesh=mesh, in_specs=in_specs, out_specs=out_specs, check_vma=False)
```

time: 368 us -> 220 us (0.60)
  waiting for transfers between devices: 222 us -> 0 us
  Pallas kernels: 0 us -> 212 us
  local copies, waits for them, and re-layouts: 48.8 us -> 5.87 us
  blocking collectives: 40.7 us -> 0 us
  matrix products: 19.3 us -> 0 us
  starting transfers between devices: 14 us -> 0 us
  between operations: 13.5 us -> 0.1 us
  other arithmetic: 7.74 us -> 1.65 us
    pallas_call x0 -> x2, Pallas kernels: none -> 212 us  [the longest x1 196 us: exchange(): pl.pallas_call(kernel, out_shape=jax.ShapeDtypeStruct((QBD * BLOCK, width...]
    all_to_all x2 -> x0, waiting for transfers between devices: 158 us -> none  [the longest x1 79.3 us: body(): lax.all_to_all(sent_keys, 'seq', split_axis=0, concat_axis=0, tiled=True)]
    reduce_scatter x1 -> x0, waiting for transfers between devices: 63.7 us -> none  [body(): lax.psum_scatter(partial_term.astype(jnp.bfloat16), 'tp', scatter_dimensi...]
    all_gather x1 -> x0, blocking collectives: 40.7 us -> none  [body(): every_list = lax.all_gather(block_lists, 'seq', axis=0, tiled=True)]
    dynamic_slice x20 -> x1, local copies, waits for them, and re-layouts: 23.5 us -> 0.01 us  [route_tables(): row = lax.dynamic_slice_in_dim(every, y * NZ, NZ, axis=0)]
    dot_general x9 -> x0, matrix products: 19.3 us -> none  [the longest x1 11.3 us: body(): jnp.dot(attended, out_weight, preferred_element_type=jnp.float32)]
    all_to_all x2 -> x0, starting transfers between devices: 14 us -> none  [the longest x1 7.85 us: body(): lax.all_to_all(sent_values, 'seq', split_axis=0, concat_axis=0, tiled=True)]
    gather x4 -> x0, local copies, waits for them, and re-layouts: 13.9 us -> none  [the longest x1 3.92 us: body(): got_keys.reshape(seq_count * slot_limit, BLOCK, kv_width)[where_from]]
  transfers between devices with their start and end apart: 3 -> 0, of which waited for: 3 -> 0; matrix products, arithmetic and copies ran while one was open for 2% -> 0% of each run, Pallas kernels for 0% -> 0%
where the time goes in v1:
time: 220 us
  Pallas kernels  212 us (96%)
  local copies, waits for them, and re-layouts  5.87 us (3%)
    pallas_call x1, Pallas kernels, exchange(): pl.pallas_call(kernel, out_shape=jax.ShapeDtypeStruct((QBD * BLOCK, width...  196 us
    pallas_call x1, Pallas kernels, gather_lists(): pl.pallas_call(lists_kernel, out_shape=jax.ShapeDtypeStruct((SEQ, 8, 128)...  16.8 us

profile of v1, /device:TPU:1, one launch (start us, length us, event | category | flops | bytes accessed | tf_op | source)
XLA Modules:
  0.0 220.0 jit_solution(5039321488376995100)
XLA Ops:
  0.0 0.8 reshape.165
  0.8 0.6 pad.4.own_ref
  1.4 16.8 %gather_lists.1 = s32[32,8,128]{2,1,0:T(8,128)} custom-call(s32[8,128]{1,0:T(8,128)} %pad.4.own_ref), custom_call_target="tpu_custom_call" | custom-call | tf_op jit(solution)/shard_map/gather_lists/pallas_call | solution.py:69
  18.2 0.9 slice.92
  19.2 0.1 broadcast_compare_fusion
  19.2 0.2 convert_reduce_fusion.1
  19.5 0.3 convert_reduce_fusion
  20.0 0.7 compare_and_fusion
  20.8 0.2 select_reduce_fusion
  21.0 1.2 concatenate.43.refs_0_
  22.2 195.6 %exchange.1 = bf16[512,1024]{1,0:T(8,128)(2,1)} custom-call(s32[12,32]{1,0:T(8,128)} %concatenate.43.refs_0_, bf16[512,512]{1,0:T(8,128)(2,1)} %refs_1_.1, bf16[512,128]{1,0:T(8,128)(2,1)} %refs_2_.1, bf16[512,128]{1,0:T(8,128)(2,1)} %refs_3_.1, bf16[32,128,128]{2,1,0:T(8,128)(2,1)} %bitcast.3, bf16[32,128,128]{2,1,0:T(8,128)(2,1)} %bitcast.4, ...), custom_call_target="tpu_custom_call" | custom-call | tf_op jit(solution)/shard_map/exchange/pallas_call | solution.py:557
  217.8 2.3 %copy.11 = bf16[512,1024]{1,0:T(8,128)(2,1)} copy(bf16[512,1024]{1,0:T(8,128)(2,1)} %exchange.1) | data formatting | bytes 2097152
  (17 shorter events, 0.2 us)

commit v2 on v1

--- a/solution.py
+++ b/solution.py
@@ -18,8 +18,9 @@
 QBD = 4
 ENT = QBD * TOPB
 G = 4
-CAPS = (8, 24, 32, 32)
-PARTS = 2
+LEVELS = ((8, 14, 18, 22), (8, 16, 24, 28), (8, 24, 32, 32))
+SPLIT = 8
+PARTS = 4
 ROWS = BLOCK // PARTS
 CHUNKS = 2 * PARTS
 MESH = pl.DeviceIdType.MESH
@@ -27,101 +28,218 @@
 BF16 = jnp.bfloat16
 
 
-def lists_kernel(own_ref, out_ref, send_sem, recv_sem):
-    me = lax.axis_index("seq")
+def plan(caps):
+    slot, direct, merge, hop = 1.31 / CHUNKS, 42.0 / CHUNKS, 0.04, 1.5
+    ready = {("z", 0, 0): 1.0, ("ya", 1): direct + hop}
+    now, link, order = 0.0, 0.0, []
+    while ready:
+        rank = {"ya": 0, "yb": 0, "z": 1, "f": 2, "s": 3}
+        due = [k for k in ready if ready[k] <= now]
+        if due:
+            step = min(due, key=lambda k: (rank[k[0]], -k[2] if k[0] == "z" else 0, k[1:]))
+        else:
+            step = min(ready, key=lambda k: (ready[k], rank[k[0]], k[1:]))
+        now = max(now, ready.pop(step))
+        order.append(step)
+        kind, ch = step[:2]
+        if kind == "ya":
+            ready["yb", ch] = now + direct / 2 + hop
+        elif kind == "yb":
+            if ch + 1 < CHUNKS:
+                ready["ya", ch + 1] = now + direct + hop
+            ready["z", ch, 0] = now
+        elif kind == "z":
+            now += 2 * caps[step[2]] * merge / PARTS
+            link = max(link, now) + caps[step[2]] * slot
+            ready[("z", ch, step[2] + 1) if step[2] < 3 else ("f", ch)] = link + hop
+        elif kind == "f":
+            now += 1.0
+            if ch == PARTS - 1:
+                for b in range(QBD):
+                    ready["s", b] = now
+        else:
+            now += 1.5
+    return order
+
+
+def total(mask, axis):
+    return jnp.sum(jnp.where(mask, 1, 0), axis=axis, keepdims=True)
+
+
+def prepare_kernel(
+    lists, kc_hbm, cols_out, tab_out, level_out, every, levels, l_send, l_recv, v_send, v_recv, y_send, y_recv, sem
+):
+    s = lax.axis_index("seq")
+    y, z = s // NZ, lax.rem(s, NZ)
+    yp = lax.rem(y + 1, NY)
+    ym = lax.rem(y + NY - 1, NY)
+
     barrier = pltpu.get_barrier_semaphore()
-
-    def greet(i, carry):
-        peer = lax.rem(me + i, SEQ)
+    ring_z = [y * NZ + lax.rem(z + i, NZ) for i in range(1, NZ)]
+    ring_y = [lax.rem(y + i, NY) * NZ + z for i in range(1, NY)]
+    for peer in ring_z + ring_y:
         pl.semaphore_signal(barrier, inc=1, device_id={"seq": peer}, device_id_type=MESH)
-        return carry
-
-    lax.fori_loop(1, SEQ, greet, 0)
-    pl.semaphore_wait(barrier, SEQ - 1)
-
-    def copy(i):
-        peer = lax.rem(me + i, SEQ)
+
+    own_rows = pl.ds(pl.multiple_of(y * SHARD, SHARD), SHARD)
+    mine = kc_hbm.at[:, pl.ds(0, ROWS), :]
+    keep = pltpu.make_async_copy(mine, cols_out.at[own_rows], sem.at[0])
+    keep.start()
+    every[z] = lists[...]
+    pl.semaphore_wait(barrier, NZ + NY - 2)
+
+    def remote(src, dst, ssem, rsem, seq):
         return pltpu.make_async_remote_copy(
-            src_ref=own_ref,
-            dst_ref=out_ref.at[me],
-            send_sem=send_sem.at[i],
-            recv_sem=recv_sem.at[i],
-            device_id={"seq": peer},
+            src_ref=src,
+            dst_ref=dst,
+            send_sem=ssem,
+            recv_sem=rsem,
+            device_id={"seq": seq},
             device_id_type=MESH,
         )
 
-    def start(i, carry):
-        copy(i).start()
-        return carry
-
-    lax.fori_loop(1, SEQ, start, 0)
-    out_ref[me] = own_ref[...]
-
-    def finish(i, carry):
-        copy(i).wait()
-        return carry
-
-    lax.fori_loop(1, SEQ, finish, 0)
-
-
-def gather_lists(block_lists):
-    padded = jnp.pad(block_lists.reshape(1, ENT), ((0, 7), (0, 128 - ENT)))
-    every = pl.pallas_call(
-        lists_kernel,
-        out_shape=jax.ShapeDtypeStruct((SEQ, 8, 128), jnp.int32),
-        in_specs=[pl.BlockSpec(memory_space=pltpu.VMEM)],
-        out_specs=pl.BlockSpec(memory_space=pltpu.VMEM),
+    told = [
+        remote(lists, every.at[z], l_send.at[i], l_recv.at[i], peer) for i, peer in enumerate(ring_z)
+    ]
+    for cp in told:
+        cp.start()
+    direct = [
+        remote(mine, cols_out.at[own_rows], y_send.at[i], y_recv.at[i], seq * NZ + z)
+        for i, seq in enumerate((yp, ym))
+    ]
+    for cp in direct:
+        cp.start()
+    for cp in told:
+        cp.wait_recv()
+
+    shape = (ENT, 128)
+    e_col = lax.broadcasted_iota(jnp.int32, shape, 0)
+    e_row = lax.broadcasted_iota(jnp.int32, shape, 1)
+    valid = e_row < ENT
+    need = jnp.zeros((1, 1), jnp.int32)
+    for k in range(NZ):
+        zk = lax.rem(z + k, NZ)
+        col = every[zk, :ENT]
+        row = jnp.broadcast_to(every[zk, ENT : ENT + 1], shape)
+        spot_col = (col >> 8) * SHARD + (col & (SHARD - 1))
+        du_col = (zk - ((col >> 5) & (NZ - 1))) & (NZ - 1)
+        du_row = (zk - ((row >> 5) & (NZ - 1))) & (NZ - 1)
+        n_up = total((du_row >= 1) & (du_row <= 3) & valid, 1)[:1]
+        n_down = total((du_row >= 5) & valid, 1)[:1]
+        n_half = total((du_row == 4) & valid, 1)[:1]
+        share = (n_half + n_down - n_up + 1) >> 1
+        share = jnp.minimum(jnp.maximum(share, n_half - SPLIT), jnp.minimum(n_half, SPLIT))
+        share = jnp.maximum(share, 0)
+        rank_col = total((e_row < e_col) & (du_row == 4) & valid, 1)
+        rank_row = total((e_col < e_row) & (du_col == 4), 0)
+
+        def routed(du, rank, bad):
+            first = rank < share
+            up = ((du >= 1) & (du <= 3)) | ((du == 4) & first)
+            down = (du >= 5) | ((du == 4) & jnp.logical_not(first))
+            way = jnp.where(up, 1, jnp.where(down, 2, 0))
+            way = jnp.where(bad, 3, way)
+            dist = jnp.where(down, NZ - du, du)
+            return way, dist
+
+        way_col, dist_col = routed(du_col, rank_col, e_row < 0)
+        way_row, dist_row = routed(du_row, rank_row, jnp.logical_not(valid))
+        order_col = (NZ - dist_col) * ENT + e_col
+        order_row = (NZ - dist_row) * ENT + e_row
+        same = way_col == way_row
+        place_col = total(same & (order_row < order_col), 1)
+
+        for i in range(4):
+            for way in (1, 2):
+                count = total((way_row == way) & (dist_row >= 4 - i), 1)[:1]
+                for level in range(len(LEVELS) - 1):
+                    over = jnp.where(count > LEVELS[level][i], level + 1, 0)
+                    need = jnp.maximum(need, over)
+
+        def pick(way, dist):
+            hit = (way_col == way) & (dist_col == dist) & (place_col == e_row)
+            return jnp.sum(jnp.where(hit, spot_col + 1, 0), axis=0, keepdims=True) - 1
+
+        if 1 <= k <= 4:
+            tab_out[4 - k : 5 - k, :] = pick(1, k)
+        if k >= 4:
+            tab_out[k : k + 1, :] = pick(2, NZ - k)
+        if k == 0:
+            place_row = total(same & (order_col < order_row), 0)
+            way = way_row[:1]
+            spot = ((row >> 8) * SHARD + (row & (SHARD - 1)))[:1]
+            tab_out[8:9, :] = way
+            tab_out[9:10, :] = jnp.where(way == 1, place_row, 0)
+            tab_out[10:11, :] = jnp.where(way == 2, place_row, 0)
+            tab_out[11:12, :] = jnp.where(way == 0, spot, 0)
+            tab_out[12:16, :] = jnp.zeros((4, 128), jnp.int32)
+
+    levels[y] = jnp.broadcast_to(need, (8, 128))
+    agree = [
+        remote(levels.at[y], levels.at[y], v_send.at[i], v_recv.at[i], peer)
+        for i, peer in enumerate(ring_y)
+    ]
+    for cp in agree:
+        cp.start()
+
+    half = SHARD // 2
+    lo = pl.ds(pl.multiple_of(ym * SHARD, SHARD), half)
+    hi = pl.ds(pl.multiple_of(yp * SHARD + half, half), half)
+    direct[0].wait_recv()
+    relay_up = remote(cols_out.at[lo], cols_out.at[lo], y_send.at[2], y_recv.at[2], yp * NZ + z)
+    relay_up.start()
+    direct[1].wait_recv()
+    relay_down = remote(cols_out.at[hi], cols_out.at[hi], y_send.at[3], y_recv.at[3], ym * NZ + z)
+    relay_down.start()
+
+    for cp in agree:
+        cp.wait_recv()
+    level_out[...] = jnp.maximum(
+        jnp.maximum(levels[0], levels[1]), jnp.maximum(levels[2], levels[3])
+    )
+    relay_up.wait_recv()
+    relay_down.wait_recv()
+    keep.wait()
+    for cp in told + direct + agree + [relay_up, relay_down]:
+        cp.wait_send()
+
+
+def prepare(block_lists, key_blocks):
+    flat = block_lists.reshape(ENT)
+    col = jnp.broadcast_to(flat[:, None], (ENT, 128))
+    row = jnp.broadcast_to(jnp.pad(flat, (0, 128 - ENT))[None], (8, 128))
+    lists = jnp.concatenate([col, row], axis=0)
+    dma = pltpu.SemaphoreType.DMA
+    vmem = pl.BlockSpec(memory_space=pltpu.VMEM)
+    any_ = pl.BlockSpec(memory_space=pl.ANY)
+    return pl.pallas_call(
+        prepare_kernel,
+        out_shape=(
+            jax.ShapeDtypeStruct((NY * SHARD, ROWS, HD), BF16),
+            jax.ShapeDtypeStruct((16, 128), jnp.int32),
+            jax.ShapeDtypeStruct((8, 128), jnp.int32),
+        ),
+        in_specs=[vmem, any_],
+        out_specs=(any_, vmem, vmem),
         scratch_shapes=[
-            pltpu.SemaphoreType.DMA((SEQ,)),
-            pltpu.SemaphoreType.DMA((SEQ,)),
+            pltpu.VMEM((NZ, ENT + 8, 128), jnp.int32),
+            pltpu.VMEM((NY, 8, 128), jnp.int32),
+            dma((NZ - 1,)),
+            dma((NZ - 1,)),
+            dma((NY - 1,)),
+            dma((NY - 1,)),
+            dma((4,)),
+            dma((4,)),
+            dma((1,)),
         ],
         compiler_params=pltpu.CompilerParams(collective_id=0, has_side_effects=True),
-        name="gather_lists",
-    )(padded)
-    return every[:, 0, :ENT]
-
-
-def route_tables(every):
-    me = lax.axis_index("seq")
-    y, z = me // NZ, me % NZ
-    row = lax.dynamic_slice_in_dim(every, y * NZ, NZ, axis=0)
-    rel = lax.dynamic_slice_in_dim(jnp.concatenate([row, row], axis=0), z, NZ, axis=0)
-    k = jnp.arange(NZ, dtype=jnp.int32)[:, None]
-    owner = rel // SHARD
-    spot = (owner // NZ) * SHARD + rel % SHARD
-    du = (z + k - owner % NZ + NZ) % NZ
-    e = jnp.arange(ENT, dtype=jnp.int32)
-    before = (e[None, :] < e[:, None])[None]
-    half = du == NZ // 2
-    rank = jnp.sum((before & half[:, None, :]).astype(jnp.int32), axis=2)
-    up = ((du >= 1) & (du <= 3)) | (half & (rank % 2 == 0))
-    down = (du >= 5) | (half & (rank % 2 == 1))
-    way = up.astype(jnp.int32) + 2 * down.astype(jnp.int32)
-    dist = jnp.where(down, NZ - du, du)
-    order = (NZ - dist) * ENT + e[None, :]
-    ahead = (way[:, None, :] == way[:, :, None]) & (order[:, None, :] < order[:, :, None])
-    place = jnp.sum(ahead.astype(jnp.int32), axis=2)
-    k_up = jnp.array([4, 3, 2, 1], jnp.int32)
-    rel_up = jnp.stack([rel_row for rel_row in (4, 3, 2, 1)]) if False else k_up
-    take = lambda a: jnp.concatenate([a[4:5], a[3:4], a[2:3], a[1:2], a[4:5], a[5:6], a[6:7], a[7:8]])
-    want_way = jnp.array([1, 1, 1, 1, 2, 2, 2, 2], jnp.int32)[:, None]
-    want_dist = jnp.concatenate([rel_up, k_up])[:, None]
-    mine = (take(way) == want_way) & (take(dist) == want_dist)
-    hit = mine[:, None, :] & (take(place)[:, None, :] == e[None, :, None])
-    steps = jnp.sum(hit.astype(jnp.int32) * (take(spot)[:, None, :] + 1), axis=2) - 1
-    last = jnp.stack(
-        [
-            way[0],
-            jnp.where(way[0] == 1, place[0], 0),
-            jnp.where(way[0] == 2, place[0], 0),
-            jnp.where(way[0] == 0, spot[0], 0),
-        ]
-    )
-    return jnp.concatenate([steps, last], axis=0)
+        name="prepare",
+    )(lists, key_blocks)
 
 
 def main_kernel(
+    caps,
     tab,
+    first_hbm,
     q_hbm,
     nk_hbm,
     nv_hbm,
@@ -195,7 +313,8 @@
         return ref.at[:, pl.ds((ch % PARTS) * ROWS, ROWS), :]
 
     own_rows = pl.ds(pl.multiple_of(y * SHARD, SHARD), SHARD)
-    own_cols = [local(source(ch), cols[ch].at[own_rows]) for ch in range(CHUNKS)]
+    own_cols = [local(first_hbm, cols[0])]
+    own_cols += [local(source(ch), cols[ch].at[own_rows]) for ch in range(1, CHUNKS)]
     in_q = local(q_hbm, q)
     in_nk = [local(nk_hbm.at[pl.ds(b * BLOCK, BLOCK)], kg.at[b, pl.ds(TOPB * BLOCK, BLOCK)]) for b in range(QBD)]
     in_nv = [local(nv_hbm.at[pl.ds(b * BLOCK, BLOCK)], vg.at[b, pl.ds(TOPB * BLOCK, BLOCK)]) for b in range(QBD)]
@@ -203,7 +322,7 @@
     pl.semaphore_wait(barrier, len(peers))
 
     half = SHARD // 2
-    y_copies = []
+    y_copies = {}
 
     def y_start(ch):
         mine = [
@@ -212,7 +331,7 @@
         ]
         for cp in mine:
             cp.start()
-        y_copies.append(mine)
+        y_copies[ch] = mine
         pending.extend(mine)
 
     def y_relay(ch):
@@ -229,11 +348,11 @@
         return a, b
 
     z_copies = {}
-    seg = 4
+    seg = 2
 
     def merge(ch, d, step):
-        cap = CAPS[step]
-        kept = CAPS[step - 1] if step else 0
+        cap = caps[step]
+        kept = caps[step - 1] if step else 0
         buf = hops[d][step][ch]
 
         def fresh(j):
@@ -259,12 +378,14 @@
             lax.fori_loop(kept // seg, cap // seg, only, 0)
 
     def z_step(ch, step):
+        if ch == 0 and step == 0:
+            own_cols[0].wait()
         for d in range(2):
             if step:
                 z_copies[ch, d, step - 1].wait_recv()
             merge(ch, d, step)
             if step < 3:
-                dst = hops[d][step + 1][ch].at[pl.ds(0, CAPS[step])]
+                dst = hops[d][step + 1][ch].at[pl.ds(0, caps[step])]
             else:
                 dst = fins[d][ch]
             cp = remote(
@@ -371,19 +492,21 @@
                 tp=sib,
             ).wait_recv()
 
-    y_start(0)
+    y_start(1)
     w_own = local(w_hbm.at[:, w_cols(t)], w_all.at[w_rows(t)])
     w_start()
 
     relays = {}
 
-    def y_finish(ch):
+    def y_first(ch):
         own_cols[ch].wait()
         relays[ch] = y_relay(ch)
+
+    def y_second(ch):
+        for cp in relays[ch]:
+            cp.wait_recv()
         if ch + 1 < CHUNKS:
             y_start(ch + 1)
-        for cp in relays[ch]:
-            cp.wait_recv()
 
     def scores(b):
         rows = pl.ds(pl.multiple_of(b * BLOCK, BLOCK), BLOCK)
@@ -391,10 +514,12 @@
         seen = TOPB * BLOCK
         row_ids = lax.broadcasted_iota(jnp.int32, (BLOCK, BLOCK), 0)
         col_ids = lax.broadcasted_iota(jnp.int32, (BLOCK, BLOCK), 1)
-        for g in range(G):
-            qt = q[rows, g * HD : (g + 1) * HD]
+
+        def head(g, carry):
+            lanes = pl.ds(pl.multiple_of(g * HD, HD), HD)
+            out = pl.ds(pl.multiple_of(g * BLOCK, BLOCK), BLOCK)
             sc = lax.dot_general(
-                qt, keys, (((1,), (1,)), ((), ())), preferred_element_type=F32
+                q[rows, lanes], keys, (((1,), (1,)), ((), ())), preferred_element_type=F32
             ) * (1.0 / math.sqrt(HD))
             near = jnp.where(col_ids <= row_ids, sc[:, seen:], -1e30)
             far = sc[:, :seen]
@@ -405,38 +530,37 @@
             en = jnp.exp(near - top)
             tot = jnp.sum(ef, axis=1, keepdims=True) + jnp.sum(en, axis=1, keepdims=True)
             inv = 1.0 / tot
-            probs[b, g * BLOCK : (g + 1) * BLOCK, :seen] = (ef * inv).astype(BF16)
-            probs[b, g * BLOCK : (g + 1) * BLOCK, seen:] = (en * inv).astype(BF16)
+            probs[b, out, :seen] = (ef * inv).astype(BF16)
+            probs[b, out, seen:] = (en * inv).astype(BF16)
+            return carry
+
+        lax.fori_loop(0, G, head, 0)
 
     def mix(b):
         o = jnp.dot(probs[b], vg[b], preferred_element_type=F32).astype(BF16)
         for g in range(G):
             att[t, b, :, g * HD : (g + 1) * HD] = o[g * BLOCK : (g + 1) * BLOCK]
 
-    forwarded = False
-    for wave in range(CHUNKS + 4):
-        for ch in range(CHUNKS):
-            step = wave - ch
-            if step < 0 or step > 4:
-                continue
-            if step == 0:
-                y_finish(ch)
-            if step < 4:
-                z_step(ch, step)
-            else:
-                collect(ch)
-                if ch == PARTS - 1:
-                    in_q.wait()
-                    for cp in in_nk:
-                        cp.wait()
-
-                    def score_step(b, carry):
-                        scores(b)
-                        return carry
-
-                    lax.fori_loop(0, QBD, score_step, 0)
-        if wave == 3:
-            w_forward()
+    seen_scores = 0
+    for step in plan(caps):
+        kind, ch = step[:2]
+        if kind == "ya":
+            y_first(ch)
+        elif kind == "yb":
+            y_second(ch)
+            if ch == CHUNKS - 1:
+                w_forward()
+        elif kind == "z":
+            z_step(ch, step[2])
+        elif kind == "f":
+            collect(ch)
+        else:
+            if not seen_scores:
+                in_q.wait()
+                for cp in in_nk:
+                    cp.wait()
+            seen_scores += 1
+            scores(ch)
 
     for cp in in_nv:
         cp.wait()
@@ -521,12 +645,13 @@
         cp.wait_send()
 
 
-def exchange(table, queries, new_keys, new_values, key_cache, value_cache, out_weight):
+def exchange(level, table, first, queries, new_keys, new_values, key_cache, value_cache, out_weight):
+    caps = LEVELS[level]
     any_ = pl.BlockSpec(memory_space=pl.ANY)
     width = out_weight.shape[1] // TP
     blk = lambda n: pltpu.VMEM((n, ROWS, HD), BF16)
-    hop_bufs = [[[blk(CAPS[i]) for _ in range(CHUNKS)] for i in range(4)] for _ in range(2)]
-    fin_bufs = [[blk(CAPS[3]) for _ in range(CHUNKS)] for _ in range(2)]
+    hop_bufs = [[[blk(caps[i]) for _ in range(CHUNKS)] for i in range(4)] for _ in range(2)]
+    fin_bufs = [[blk(caps[3]) for _ in range(CHUNKS)] for _ in range(2)]
     scratch = [
         [blk(NY * SHARD) for _ in range(CHUNKS)],
         hop_bufs,
@@ -549,36 +674,50 @@
         pltpu.SemaphoreType.DMA((CHUNKS + 2 + 2 * QBD,)),
     ]
     flat, tree = jax.tree.flatten(scratch)
-    fixed = 8
+    fixed = 9
 
     def kernel(*refs):
-        main_kernel(*refs[:fixed], *jax.tree.unflatten(tree, refs[fixed:]))
+        main_kernel(caps, *refs[:fixed], *jax.tree.unflatten(tree, refs[fixed:]))
 
     return pl.pallas_call(
         kernel,
         out_shape=jax.ShapeDtypeStruct((QBD * BLOCK, width), BF16),
-        in_specs=[pl.BlockSpec(memory_space=pltpu.SMEM)] + [any_] * 6,
+        in_specs=[pl.BlockSpec(memory_space=pltpu.SMEM)] + [any_] * 7,
         out_specs=pl.BlockSpec(memory_space=pltpu.VMEM),
         scratch_shapes=flat,
         compiler_params=pltpu.CompilerParams(
-            collective_id=1, has_side_effects=True, vmem_limit_bytes=60 * 1024 * 1024
+            collective_id=1 + level, has_side_effects=True, vmem_limit_bytes=60 * 1024 * 1024
         ),
         name="exchange",
     )(
         table,
+        first,
         queries,
         new_keys,
         new_values,
-        key_cache.reshape(SHARD, BLOCK, HD),
-        value_cache.reshape(SHARD, BLOCK, HD),
+        key_cache,
+        value_cache,
         out_weight,
     )
 
 
 def body(queries, new_keys, new_values, key_cache, value_cache, block_lists, out_weight):
-    every = gather_lists(block_lists)
-    table = route_tables(every)
-    return exchange(table, queries, new_keys, new_values, key_cache, value_cache, out_weight)
+    key_blocks = key_cache.reshape(SHARD, BLOCK, HD)
+    value_blocks = value_cache.reshape(SHARD, BLOCK, HD)
+    first, table, level = prepare(block_lists, key_blocks)
+    branches = [functools.partial(exchange, i) for i in range(len(LEVELS))]
+    return lax.switch(
+        level[0, 0],
+        branches,
+        table,
+        first,
+        queries,
+        new_keys,
+        new_values,
+        key_blocks,
+        value_blocks,
+        out_weight,
+    )
 
 
 def solution(mesh):

time: 220 us -> 166 us (0.75)
  Pallas kernels: 212 us -> 161 us
  local copies, waits for them, and re-layouts: 5.87 us -> 2.94 us
    pallas_call x1, Pallas kernels: 196 us -> 140 us  [exchange(): pl.pallas_call(kernel, out_shape=jax.ShapeDtypeStruct((QBD * BLOCK, width...]
    pallas_call x1, Pallas kernels: 16.8 us -> 20.9 us  [prepare(): pl.pallas_call(prepare_kernel, out_shape=(jax.ShapeDtypeStruct((NY * SHAR...]
where the time goes in v2:
time: 166 us; the launch traced here: 165 us
  Pallas kernels  161 us (97%)
  local copies, waits for them, and re-layouts  2.94 us (2%)
    pallas_call x1, Pallas kernels, exchange(): pl.pallas_call(kernel, out_shape=jax.ShapeDtypeStruct((QBD * BLOCK, width...  140 us
    pallas_call x1, Pallas kernels, prepare(): pl.pallas_call(prepare_kernel, out_shape=(jax.ShapeDtypeStruct((NY * SHAR...  20.9 us

profile of v2, /device:TPU:1, one launch (start us, length us, event | category | flops | bytes accessed | tf_op | source)
XLA Modules:
  0.0 165.5 jit_solution(2385186798153253938)
XLA Ops:
  0.0 0.8 reshape.14
  0.8 0.7 pad_add_fusion.lists
  1.5 20.9 %prepare.1 = (bf16[128,32,128]{2,1,0:T(8,128)(2,1)S(1)}, s32[16,128]{1,0:T(8,128)S(1)}, s32[8,128]{1,0:T(8,128)}) custom-call(s32[40,128]{1,0:T(8,128)} %pad_add_fusion.lists, bf16[32,128,128]{2,1,0:T(8,128)(2,1)} %bitcast.3), custom_call_target="tpu_custom_call" | custom-call | tf_op jit(solution)/shard_map/prepare/pallas_call | solution.py:214
  22.4 1.2 slice.3
  24.2 140.3 %conditional.1 = (bf16[512,1024]{1,0:T(8,128)(2,1)S(1)}) conditional(s32[]{:T(128)} %bitcast.1, (s32[16,128]{1,0:T(8,128)S(1)}, bf16[128,32,128]{2,1,0:T(8,128)(2,1)S(1)}, bf16[512,512]{1,0:T(8,128)(2,1)}, bf16[512,128]{1,0:T(8,128)(2,1)}, bf16[512,128]{1,0:T(8,128)(2,1)}, /*index=5*/bf16[32,128,128]{2,1,0:T(8,128)(2,1)}, ...), branch_computations={%region_0.1_spmd, %region_1.2_spmd, %region_2.3_spmd} | conditional | bytes 8 | solution.py:709
  24.2 140.0 %exchange.3 = bf16[512,1024]{1,0:T(8,128)(2,1)S(1)} custom-call(s32[16,128]{1,0:T(8,128)S(1)} %get-tuple-element.56.refs_0_, bf16[128,32,128]{2,1,0:T(8,128)(2,1)S(1)} %get-tuple-element.58.refs_1_, bf16[512,512]{1,0:T(8,128)(2,1)} %get-tuple-element.59.refs_2_, bf16[512,128]{1,0:T(8,128)(2,1)} %get-tuple-element.60.refs_3_, ...), custom_call_target="tpu_custom_call" | custom-call | tf_op jit(solution)/shard_map/cond/branch_0_fun/exchange/pallas_call | solution.py:682
  164.5 1.0 copy.15
  (3 shorter events, 0.0 us)

commit v3 on v2

--- a/solution.py
+++ b/solution.py
@@ -28,38 +28,102 @@
 BF16 = jnp.bfloat16
 
 
-def plan(caps):
-    slot, direct, merge, hop = 1.31 / CHUNKS, 42.0 / CHUNKS, 0.04, 1.5
-    ready = {("z", 0, 0): 1.0, ("ya", 1): direct + hop}
-    now, link, order = 0.0, 0.0, []
-    while ready:
-        rank = {"ya": 0, "yb": 0, "z": 1, "f": 2, "s": 3}
-        due = [k for k in ready if ready[k] <= now]
-        if due:
-            step = min(due, key=lambda k: (rank[k[0]], -k[2] if k[0] == "z" else 0, k[1:]))
-        else:
-            step = min(ready, key=lambda k: (ready[k], rank[k[0]], k[1:]))
-        now = max(now, ready.pop(step))
-        order.append(step)
-        kind, ch = step[:2]
-        if kind == "ya":
-            ready["yb", ch] = now + direct / 2 + hop
-        elif kind == "yb":
-            if ch + 1 < CHUNKS:
-                ready["ya", ch + 1] = now + direct + hop
-            ready["z", ch, 0] = now
-        elif kind == "z":
-            now += 2 * caps[step[2]] * merge / PARTS
-            link = max(link, now) + caps[step[2]] * slot
-            ready[("z", ch, step[2] + 1) if step[2] < 3 else ("f", ch)] = link + hop
-        elif kind == "f":
-            now += 1.0
-            if ch == PARTS - 1:
-                for b in range(QBD):
-                    ready["s", b] = now
-        else:
-            now += 1.5
-    return order
+ORDER = (
+    ("z", 0, 0),
+    ("v", 0),
+    ("z", 0, 1),
+    ("v", 1),
+    ("v", 2),
+    ("ya", 1),
+    ("yb", 1),
+    ("z", 1, 0),
+    ("z", 0, 2),
+    ("ya", 2),
+    ("v", 3),
+    ("z", 0, 3),
+    ("yb", 2),
+    ("z", 2, 0),
+    ("z", 1, 1),
+    ("z", 2, 1),
+    ("ya", 3),
+    ("f", 0),
+    ("z", 1, 2),
+    ("yb", 3),
+    ("z", 3, 0),
+    ("z", 2, 2),
+    ("z", 3, 1),
+    ("ya", 4),
+    ("z", 2, 3),
+    ("yb", 4),
+    ("z", 1, 3),
+    ("z", 4, 0),
+    ("f", 2),
+    ("z", 3, 2),
+    ("ya", 5),
+    ("z", 4, 1),
+    ("f", 1),
+    ("yb", 5),
+    ("z", 5, 0),
+    ("z", 3, 3),
+    ("z", 5, 1),
+    ("ya", 6),
+    ("z", 4, 2),
+    ("f", 3),
+    ("s", 0),
+    ("yb", 6),
+    ("z", 6, 0),
+    ("z", 5, 2),
+    ("z", 6, 1),
+    ("ya", 7),
+    ("z", 4, 3),
+    ("s", 1),
+    ("yb", 7),
+    ("z", 7, 0),
+    ("z", 5, 3),
+    ("z", 7, 1),
+    ("s", 2),
+    ("z", 6, 2),
+    ("f", 4),
+    ("s", 3),
+    ("f", 5),
+    ("z", 7, 2),
+    ("A", 0, 0),
+    ("z", 6, 3),
+    ("A", 0, 1),
+    ("A", 0, 2),
+    ("B", 0, 0),
+    ("z", 7, 3),
+    ("A", 0, 3),
+    ("B", 0, 1),
+    ("f", 6),
+    ("B", 0, 3),
+    ("C", 0, 0),
+    ("C", 0, 1),
+    ("B", 0, 2),
+    ("f", 7),
+    ("A", 1, 0),
+    ("A", 1, 1),
+    ("A", 1, 2),
+    ("A", 1, 3),
+    ("D", 0, 1),
+    ("B", 1, 0),
+    ("C", 0, 2),
+    ("B", 1, 1),
+    ("D", 0, 0),
+    ("B", 1, 2),
+    ("C", 0, 3),
+    ("B", 1, 3),
+    ("C", 1, 0),
+    ("C", 1, 1),
+    ("D", 0, 2),
+    ("C", 1, 2),
+    ("D", 0, 3),
+    ("C", 1, 3),
+    ("D", 1, 0),
+    ("D", 1, 1),
+    ("D", 1, 2),
+    ("D", 1, 3),
+)
 
 
 def total(mask, axis):
@@ -257,6 +321,9 @@
     att,
     w_all,
     w_relay,
+    acc,
+    v_own,
+    v_new,
     y_send,
     y_recv,
     z_send,
@@ -309,15 +376,17 @@
         return cp
 
     def source(ch):
-        ref = kc_hbm if ch < PARTS else vc_hbm
-        return ref.at[:, pl.ds((ch % PARTS) * ROWS, ROWS), :]
+        if ch < PARTS:
+            return kc_hbm.at[:, pl.ds(ch * ROWS, ROWS), :]
+        return cols[ch].at[own_rows]
 
     own_rows = pl.ds(pl.multiple_of(y * SHARD, SHARD), SHARD)
     own_cols = [local(first_hbm, cols[0])]
-    own_cols += [local(source(ch), cols[ch].at[own_rows]) for ch in range(1, CHUNKS)]
+    own_cols += [local(source(ch), cols[ch].at[own_rows]) for ch in range(1, PARTS)]
+    in_v = local(vc_hbm, v_own)
     in_q = local(q_hbm, q)
     in_nk = [local(nk_hbm.at[pl.ds(b * BLOCK, BLOCK)], kg.at[b, pl.ds(TOPB * BLOCK, BLOCK)]) for b in range(QBD)]
-    in_nv = [local(nv_hbm.at[pl.ds(b * BLOCK, BLOCK)], vg.at[b, pl.ds(TOPB * BLOCK, BLOCK)]) for b in range(QBD)]
+    in_nv = local(nv_hbm, v_new)
 
     pl.semaphore_wait(barrier, len(peers))
 
@@ -402,7 +471,6 @@
     def collect(ch):
         for d in range(2):
             z_copies[ch, d, 3].wait_recv()
-        dst = kg if ch < PARTS else vg
         r0 = (ch % PARTS) * ROWS
         for b in range(QBD):
 
@@ -414,20 +482,36 @@
                     cols[ch][tab[11, e]],
                     jnp.where(way == 1, fins[0][ch][tab[9, e]], fins[1][ch][tab[10, e]]),
                 )
-                dst[b, pl.ds(pl.multiple_of(i * BLOCK + r0, ROWS), ROWS), :] = val
+                at = pl.multiple_of(i * BLOCK, BLOCK)
+                if ch < PARTS:
+                    kg[b, pl.ds(at + r0, ROWS), :] = val
+                else:
+                    vg[b, pl.ds(r0, ROWS), pl.ds(at, BLOCK)] = val
                 return carry
 
             lax.fori_loop(0, TOPB, entry, 0)
 
-    depth = G * HD
-    width = w_hbm.shape[1] // TP
-    hd = depth // 2
+    def turn(i):
+        if i == 0:
+            in_v.wait()
+            in_nv.wait()
+        n = SHARD // QBD
+
+        def block(j, carry):
+            blk = i * n + j
+            flipped = v_own[blk].T
+            for p in range(PARTS):
+                cols[PARTS + p][y * SHARD + blk] = flipped[p * ROWS : (p + 1) * ROWS]
+            return carry
+
+        lax.fori_loop(0, n, block, 0)
+        vg[i, :, TOPB * BLOCK :] = v_new[i * BLOCK : (i + 1) * BLOCK, :].T
+
+    width = w_hbm.shape[3] // TP
+    hg = G // 2
 
     def w_cols(tt):
         return pl.ds(pl.multiple_of(tt * width, width), width)
-
-    def w_rows(tt, off=0, n=depth):
-        return pl.ds(pl.multiple_of(tt * depth + off, hd), n)
 
     w_direct, w_first = [], []
 
@@ -437,7 +521,7 @@
         for dirn in range(2):
             for cc in range(NC):
                 cp = remote(
-                    w_hbm.at[pl.ds(dirn * hd, hd), w_cols(xo * NC + cc)],
+                    w_hbm.at[pl.ds(dirn * hg, hg), :, :, w_cols(xo * NC + cc)],
                     w_relay.at[dirn * NC + cc],
                     w_send.at[5 + dirn * NC + cc],
                     w_recv.at[5 + dirn * NC + cc],
@@ -448,8 +532,8 @@
                 pending.append(cp)
         for i, (tt, slot) in enumerate(zip(targets, slots)):
             cp = remote(
-                w_hbm.at[:, w_cols(tt)],
-                w_all.at[w_rows(t)],
+                w_hbm.at[:, :, :, w_cols(tt)],
+                w_all.at[t],
                 w_send.at[i],
                 w_recv.at[slot],
                 tp=tt,
@@ -466,10 +550,9 @@
                 w_first[dirn * NC + cc].wait_recv()
                 src_t = (xm if dirn == 0 else xp) * NC + c
                 dst_t = (xp if dirn == 0 else xm) * NC + cc
-                rows = w_rows(src_t, dirn * hd, hd)
                 cp = remote(
                     w_relay.at[dirn * NC + cc],
-                    w_all.at[rows],
+                    w_all.at[src_t, pl.ds(dirn * hg, hg)],
                     w_send.at[9 + dirn * NC + cc],
                     w_recv.at[9 + dirn * NC + c],
                     tp=dst_t,
@@ -481,32 +564,33 @@
     def w_wait():
         for slot in range(5):
             remote(
-                w_hbm.at[:, w_cols(t)], w_all.at[w_rows(t)], w_send.at[0], w_recv.at[slot], tp=sib
+                w_hbm.at[:, :, :, w_cols(t)], w_all.at[t], w_send.at[0], w_recv.at[slot], tp=sib
             ).wait_recv()
         for slot in range(4):
             remote(
                 w_relay.at[slot],
-                w_all.at[w_rows(t, 0, hd)],
+                w_all.at[t, pl.ds(0, hg)],
                 w_send.at[9],
                 w_recv.at[9 + slot],
                 tp=sib,
             ).wait_recv()
 
     y_start(1)
-    w_own = local(w_hbm.at[:, w_cols(t)], w_all.at[w_rows(t)])
+    w_own = local(w_hbm.at[:, :, :, w_cols(t)], w_all.at[t])
     w_start()
 
     relays = {}
 
     def y_first(ch):
-        own_cols[ch].wait()
+        if ch < PARTS:
+            own_cols[ch].wait()
         relays[ch] = y_relay(ch)
+        if ch + 1 < CHUNKS:
+            y_start(ch + 1)
 
     def y_second(ch):
         for cp in relays[ch]:
             cp.wait_recv()
-        if ch + 1 < CHUNKS:
-            y_start(ch + 1)
 
     def scores(b):
         rows = pl.ds(pl.multiple_of(b * BLOCK, BLOCK), BLOCK)
@@ -536,110 +620,125 @@
 
         lax.fori_loop(0, G, head, 0)
 
-    def mix(b):
-        o = jnp.dot(probs[b], vg[b], preferred_element_type=F32).astype(BF16)
+    half_d = HD // 2
+
+    def mix(h, b):
+        values = vg[b, h * half_d : (h + 1) * half_d, :]
         for g in range(G):
-            att[t, b, :, g * HD : (g + 1) * HD] = o[g * BLOCK : (g + 1) * BLOCK]
+            o = lax.dot_general(
+                probs[b, g * BLOCK : (g + 1) * BLOCK, :],
+                values,
+                (((1,), (1,)), ((), ())),
+                preferred_element_type=F32,
+            )
+            att[t, h, b, :, g * half_d : (g + 1) * half_d] = o.astype(BF16)
+
+    hb = BLOCK // 2
+    a_first, a_second, a_third = {}, {}, {}
+
+    def sem(k, i):
+        return a_send.at[k[0] * QBD + k[1], i], a_recv.at[k[0] * QBD + k[1], i]
+
+    def stage_a(*k):
+        mix(*k)
+        own = att.at[t, k[0], k[1]]
+        cps = [
+            remote(own, own, *sem(k, i), tp=tt)
+            for i, tt in enumerate((xp * NC + c, xm * NC + c, sib))
+        ]
+        for cp in cps:
+            cp.start()
+        a_first[k] = cps
+        pending.extend(cps)
+
+    lo, hi = pl.ds(0, hb), pl.ds(hb, hb)
+
+    def stage_b(*k):
+        tm, tpl = xm * NC + c, xp * NC + c
+        got = att.at[tm, k[0], k[1]]
+        a_first[k][0].wait_recv()
+        cps = [
+            remote(got.at[lo], got.at[lo], *sem(k, 3), tp=tpl),
+            remote(got, got, *sem(k, 4), tp=sib),
+        ]
+        for cp in cps:
+            cp.start()
+        got = att.at[tpl, k[0], k[1]]
+        a_first[k][1].wait_recv()
+        more = [
+            remote(got.at[hi], got.at[hi], *sem(k, 5), tp=tm),
+            remote(got, got, *sem(k, 6), tp=sib),
+        ]
+        for cp in more:
+            cp.start()
+        a_second[k] = cps + more
+        pending.extend(a_second[k])
+
+    def stage_c(*k):
+        got = att.at[xo * NC + c, k[0], k[1]]
+        a_second[k][0].wait_recv()
+        a_second[k][2].wait_recv()
+        cp = remote(got, got, *sem(k, 7), tp=sib)
+        cp.start()
+        a_third[k] = cp
+        pending.append(cp)
+
+    w_ready = []
+
+    def stage_d(*k):
+        h, b = k
+        if not w_ready:
+            w_ready.append(True)
+            w_own.wait()
+            w_wait()
+        a_first[k][2].wait_recv()
+        a_second[k][1].wait_recv()
+        a_second[k][3].wait_recv()
+        a_third[k].wait_recv()
+        rows = slice(b * BLOCK, (b + 1) * BLOCK)
+        if not h:
+            acc[rows, :] = jnp.zeros((BLOCK, width), F32)
+
+            def term(tt, carry):
+                weights = w_all[tt, :, h].reshape(G * half_d, width)
+                acc[rows, :] += jnp.dot(att[tt, h, b], weights, preferred_element_type=F32)
+                return carry
+
+            lax.fori_loop(0, TP, term, 0)
+        else:
+            part = acc[rows, :]
+            for tt in range(TP):
+                part += jnp.dot(
+                    att[tt, h, b],
+                    w_all[tt, :, h].reshape(G * half_d, width),
+                    preferred_element_type=F32,
+                )
+            out_ref[rows, :] = part.astype(BF16)
 
     seen_scores = 0
-    for step in plan(caps):
+    for step in ORDER:
         kind, ch = step[:2]
         if kind == "ya":
             y_first(ch)
         elif kind == "yb":
             y_second(ch)
-            if ch == CHUNKS - 1:
+            if ch == 3:
                 w_forward()
         elif kind == "z":
             z_step(ch, step[2])
         elif kind == "f":
             collect(ch)
-        else:
+        elif kind == "v":
+            turn(ch)
+        elif kind == "s":
             if not seen_scores:
                 in_q.wait()
                 for cp in in_nk:
                     cp.wait()
             seen_scores += 1
             scores(ch)
-
-    for cp in in_nv:
-        cp.wait()
-
-    hb = BLOCK // 2
-    a_first, a_second, a_third = {}, {}, {}
-
-    def sem(b, i):
-        return a_send.at[b, i], a_recv.at[b, i]
-
-    def stage_a(b):
-        mix(b)
-        cps = [
-            remote(att.at[t, b], att.at[t, b], *sem(b, i), tp=tt)
-            for i, tt in enumerate((xp * NC + c, xm * NC + c, sib))
-        ]
-        for cp in cps:
-            cp.start()
-        a_first[b] = cps
-        pending.extend(cps)
-
-    lo, hi = pl.ds(0, hb), pl.ds(hb, hb)
-
-    def stage_b(b):
-        tm, tpl = xm * NC + c, xp * NC + c
-        a_first[b][0].wait_recv()
-        cps = [
-            remote(att.at[tm, b, lo], att.at[tm, b, lo], *sem(b, 3), tp=tpl),
-            remote(att.at[tm, b], att.at[tm, b], *sem(b, 4), tp=sib),
-        ]
-        for cp in cps:
-            cp.start()
-        a_first[b][1].wait_recv()
-        more = [
-            remote(att.at[tpl, b, hi], att.at[tpl, b, hi], *sem(b, 5), tp=tm),
-            remote(att.at[tpl, b], att.at[tpl, b], *sem(b, 6), tp=sib),
-        ]
-        for cp in more:
-            cp.start()
-        a_second[b] = cps + more
-        pending.extend(a_second[b])
-
-    def stage_c(b):
-        to = xo * NC + c
-        a_second[b][0].wait_recv()
-        a_second[b][2].wait_recv()
-        cp = remote(att.at[to, b], att.at[to, b], *sem(b, 7), tp=sib)
-        cp.start()
-        a_third[b] = cp
-        pending.append(cp)
-
-    def stage_d(b):
-        a_first[b][2].wait_recv()
-        a_second[b][1].wait_recv()
-        a_second[b][3].wait_recv()
-        a_third[b].wait_recv()
-        acc = jnp.zeros((BLOCK, width), F32)
-        for tt in range(TP):
-            acc += jnp.dot(
-                att[tt, b], w_all[tt * depth : (tt + 1) * depth, :], preferred_element_type=F32
-            )
-        out_ref[b * BLOCK : (b + 1) * BLOCK, :] = acc.astype(BF16)
-
-    for b in range(QBD):
-        stage_a(b)
-    w_own.wait()
-    w_wait()
-    stage_b(0)
-    stage_b(1)
-    stage_c(0)
-    stage_b(2)
-    stage_c(1)
-    stage_d(0)
-    stage_b(3)
-    stage_c(2)
-    stage_d(1)
-    stage_c(3)
-    stage_d(2)
-    stage_d(3)
+        else:
+            {"A": stage_a, "B": stage_b, "C": stage_c, "D": stage_d}[kind](ch, step[2])
 
     for cp in pending:
         cp.wait_send()
@@ -648,7 +747,7 @@
 def exchange(level, table, first, queries, new_keys, new_values, key_cache, value_cache, out_weight):
     caps = LEVELS[level]
     any_ = pl.BlockSpec(memory_space=pl.ANY)
-    width = out_weight.shape[1] // TP
+    width = out_weight.shape[3] // TP
     blk = lambda n: pltpu.VMEM((n, ROWS, HD), BF16)
     hop_bufs = [[[blk(caps[i]) for _ in range(CHUNKS)] for i in range(4)] for _ in range(2)]
     fin_bufs = [[blk(caps[3]) for _ in range(CHUNKS)] for _ in range(2)]
@@ -657,21 +756,24 @@
         hop_bufs,
         fin_bufs,
         pltpu.VMEM((QBD, (TOPB + 1) * BLOCK, HD), BF16),
-        pltpu.VMEM((QBD, (TOPB + 1) * BLOCK, HD), BF16),
+        pltpu.VMEM((QBD, HD, (TOPB + 1) * BLOCK), BF16),
         pltpu.VMEM((QBD * BLOCK, G * HD), BF16),
         pltpu.VMEM((QBD, G * BLOCK, (TOPB + 1) * BLOCK), BF16),
-        pltpu.VMEM((TP, QBD, BLOCK, G * HD), BF16),
-        pltpu.VMEM((TP * G * HD, width), BF16),
-        pltpu.VMEM((4, G * HD // 2, width), BF16),
+        pltpu.VMEM((TP, 2, QBD, BLOCK, G * HD // 2), BF16),
+        pltpu.VMEM((TP, G, 2, HD // 2, width), BF16),
+        pltpu.VMEM((4, G // 2, 2, HD // 2, width), BF16),
+        pltpu.VMEM((QBD * BLOCK, width), F32),
+        pltpu.VMEM((SHARD, BLOCK, HD), BF16),
+        pltpu.VMEM((QBD * BLOCK, HD), BF16),
         pltpu.SemaphoreType.DMA((CHUNKS, 4)),
         pltpu.SemaphoreType.DMA((CHUNKS, 4)),
         pltpu.SemaphoreType.DMA((CHUNKS, 2, 4)),
         pltpu.SemaphoreType.DMA((CHUNKS, 2, 4)),
         pltpu.SemaphoreType.DMA((13,)),
         pltpu.SemaphoreType.DMA((13,)),
-        pltpu.SemaphoreType.DMA((QBD, 8)),
-        pltpu.SemaphoreType.DMA((QBD, 8)),
-        pltpu.SemaphoreType.DMA((CHUNKS + 2 + 2 * QBD,)),
+        pltpu.SemaphoreType.DMA((2 * QBD, 8)),
+        pltpu.SemaphoreType.DMA((2 * QBD, 8)),
+        pltpu.SemaphoreType.DMA((PARTS + 4 + QBD,)),
     ]
     flat, tree = jax.tree.flatten(scratch)
     fixed = 9
@@ -716,7 +818,7 @@
         new_values,
         key_blocks,
         value_blocks,
-        out_weight,
+        out_weight.reshape(G, 2, HD // 2, -1),
     )
 
 

time: 166 us -> 151 us (0.910)
  Pallas kernels: 161 us -> 146 us
    pallas_call x1, Pallas kernels: 140 us -> 125 us  [exchange(): pl.pallas_call(kernel, out_shape=jax.ShapeDtypeStruct((QBD * BLOCK, width...]
where the time goes in v3:
time: 151 us
  Pallas kernels  146 us (97%)
  local copies, waits for them, and re-layouts  2.94 us (2%)
    pallas_call x1, Pallas kernels, exchange(): pl.pallas_call(kernel, out_shape=jax.ShapeDtypeStruct((QBD * BLOCK, width...  125 us
    pallas_call x1, Pallas kernels, prepare(): pl.pallas_call(prepare_kernel, out_shape=(jax.ShapeDtypeStruct((NY * SHAR...  20.9 us

profile of v3, /device:TPU:1, one launch (start us, length us, event | category | flops | bytes accessed | tf_op | source)
XLA Modules:
  0.0 150.8 jit_solution(290255397308559385)
XLA Ops:
  0.0 0.8 reshape.18
  0.8 0.7 pad_add_fusion.lists
  1.5 20.9 %prepare.1 = (bf16[128,32,128]{2,1,0:T(8,128)(2,1)S(1)}, s32[16,128]{1,0:T(8,128)S(1)}, s32[8,128]{1,0:T(8,128)}) custom-call(s32[40,128]{1,0:T(8,128)} %pad_add_fusion.lists, bf16[32,128,128]{2,1,0:T(8,128)(2,1)} %bitcast.7), custom_call_target="tpu_custom_call" | custom-call | tf_op jit(solution)/shard_map/prepare/pallas_call | solution.py:278
  22.4 1.2 slice.3
  24.2 125.6 %conditional.1 = (bf16[512,1024]{1,0:T(8,128)(2,1)S(1)}) conditional(s32[]{:T(128)} %bitcast.1, (s32[16,128]{1,0:T(8,128)S(1)}, bf16[128,32,128]{2,1,0:T(8,128)(2,1)S(1)}, bf16[512,512]{1,0:T(8,128)(2,1)}, bf16[512,128]{1,0:T(8,128)(2,1)}, bf16[512,128]{1,0:T(8,128)(2,1)}, /*index=5*/bf16[32,128,128]{2,1,0:T(8,128)(2,1)}, ...), branch_computations={%region_0.1_spmd, %region_1.2_spmd, %region_2.3_spmd} | conditional | bytes 8 | solution.py:811
  24.2 125.4 %exchange.3 = bf16[512,1024]{1,0:T(8,128)(2,1)S(1)} custom-call(s32[16,128]{1,0:T(8,128)S(1)} %get-tuple-element.56.refs_0_, bf16[128,32,128]{2,1,0:T(8,128)(2,1)S(1)} %get-tuple-element.58.refs_1_, bf16[512,512]{1,0:T(8,128)(2,1)} %get-tuple-element.59.refs_2_, bf16[512,128]{1,0:T(8,128)(2,1)} %get-tuple-element.60.refs_3_, ...), custom_call_target="tpu_custom_call" | custom-call | tf_op jit(solution)/shard_map/cond/branch_0_fun/exchange/pallas_call | solution.py:784
  149.8 1.0 copy.15
  (3 shorter events, 0.0 us)

commit v4 on v3

--- a/solution.py
+++ b/solution.py
@@ -18,7 +18,7 @@
 QBD = 4
 ENT = QBD * TOPB
 G = 4
-LEVELS = ((8, 14, 18, 22), (8, 16, 24, 28), (8, 24, 32, 32))
+LEVELS = ((8, 14, 18, 22), (8, 16, 22, 26), (8, 24, 32, 32))
 SPLIT = 8
 PARTS = 4
 ROWS = BLOCK // PARTS
@@ -91,8 +91,8 @@
     ("z", 6, 3),
     ("A", 0, 1),
     ("A", 0, 2),
+    ("z", 7, 3),
     ("B", 0, 0),
-    ("z", 7, 3),
     ("A", 0, 3),
     ("B", 0, 1),
     ("f", 6),
@@ -166,12 +166,29 @@
     ]
     for cp in told:
         cp.start()
-    direct = [
-        remote(mine, cols_out.at[own_rows], y_send.at[i], y_recv.at[i], seq * NZ + z)
-        for i, seq in enumerate((yp, ym))
-    ]
-    for cp in direct:
-        cp.start()
+    half = SHARD // 2
+    direct = []
+    for turn in range(2):
+        for i, seq in enumerate((yp, ym)):
+            part = (i + turn) % 2
+            rows = pl.ds(pl.multiple_of(y * SHARD + part * half, half), half)
+            cp = remote(
+                kc_hbm.at[pl.ds(part * half, half), pl.ds(0, ROWS), :],
+                cols_out.at[rows],
+                y_send.at[2 * turn + i],
+                y_recv.at[2 * turn + i],
+                seq * NZ + z,
+            )
+            cp.start()
+            direct.append(cp)
+    lo = pl.ds(pl.multiple_of(ym * SHARD, half), half)
+    hi = pl.ds(pl.multiple_of(yp * SHARD + half, half), half)
+    direct[0].wait_recv()
+    relay_up = remote(cols_out.at[lo], cols_out.at[lo], y_send.at[4], y_recv.at[4], yp * NZ + z)
+    relay_up.start()
+    direct[1].wait_recv()
+    relay_down = remote(cols_out.at[hi], cols_out.at[hi], y_send.at[5], y_recv.at[5], ym * NZ + z)
+    relay_down.start()
     for cp in told:
         cp.wait_recv()
 
@@ -245,23 +262,13 @@
     for cp in agree:
         cp.start()
 
-    half = SHARD // 2
-    lo = pl.ds(pl.multiple_of(ym * SHARD, SHARD), half)
-    hi = pl.ds(pl.multiple_of(yp * SHARD + half, half), half)
-    direct[0].wait_recv()
-    relay_up = remote(cols_out.at[lo], cols_out.at[lo], y_send.at[2], y_recv.at[2], yp * NZ + z)
-    relay_up.start()
-    direct[1].wait_recv()
-    relay_down = remote(cols_out.at[hi], cols_out.at[hi], y_send.at[3], y_recv.at[3], ym * NZ + z)
-    relay_down.start()
-
     for cp in agree:
         cp.wait_recv()
     level_out[...] = jnp.maximum(
         jnp.maximum(levels[0], levels[1]), jnp.maximum(levels[2], levels[3])
     )
-    relay_up.wait_recv()
-    relay_down.wait_recv()
+    for cp in (direct[2], direct[3], relay_up, relay_down):
+        cp.wait_recv()
     keep.wait()
     for cp in told + direct + agree + [relay_up, relay_down]:
         cp.wait_send()
@@ -291,8 +298,8 @@
             dma((NZ - 1,)),
             dma((NY - 1,)),
             dma((NY - 1,)),
-            dma((4,)),
-            dma((4,)),
+            dma((6,)),
+            dma((6,)),
             dma((1,)),
         ],
         compiler_params=pltpu.CompilerParams(collective_id=0, has_side_effects=True),

time: 151 us -> 150 us (level)
  no operation moved by 1% of the time
where the time goes in v4:
time: 150 us
  Pallas kernels  145 us (97%)
  local copies, waits for them, and re-layouts  2.94 us (2%)
    pallas_call x1, Pallas kernels, exchange(): pl.pallas_call(kernel, out_shape=jax.ShapeDtypeStruct((QBD * BLOCK, width...  124 us
    pallas_call x1, Pallas kernels, prepare(): pl.pallas_call(prepare_kernel, out_shape=(jax.ShapeDtypeStruct((NY * SHAR...  20.9 us

profile of v4, /device:TPU:1, one launch (start us, length us, event | category | flops | bytes accessed | tf_op | source)
XLA Modules:
  0.0 150.0 jit_solution(8015556545055254105)
XLA Ops:
  0.0 0.8 reshape.18
  0.8 0.7 pad_add_fusion.lists
  1.5 20.9 %prepare.1 = (bf16[128,32,128]{2,1,0:T(8,128)(2,1)S(1)}, s32[16,128]{1,0:T(8,128)S(1)}, s32[8,128]{1,0:T(8,128)}) custom-call(s32[40,128]{1,0:T(8,128)} %pad_add_fusion.lists, bf16[32,128,128]{2,1,0:T(8,128)(2,1)} %bitcast.7), custom_call_target="tpu_custom_call" | custom-call | tf_op jit(solution)/shard_map/prepare/pallas_call | solution.py:285
  22.4 1.2 slice.3
  24.3 124.7 %conditional.1 = (bf16[512,1024]{1,0:T(8,128)(2,1)S(1)}) conditional(s32[]{:T(128)} %bitcast.1, (s32[16,128]{1,0:T(8,128)S(1)}, bf16[128,32,128]{2,1,0:T(8,128)(2,1)S(1)}, bf16[512,512]{1,0:T(8,128)(2,1)}, bf16[512,128]{1,0:T(8,128)(2,1)}, bf16[512,128]{1,0:T(8,128)(2,1)}, /*index=5*/bf16[32,128,128]{2,1,0:T(8,128)(2,1)}, ...), branch_computations={%region_0.1_spmd, %region_1.2_spmd, %region_2.3_spmd} | conditional | bytes 8 | solution.py:818
  24.3 124.5 %exchange.3 = bf16[512,1024]{1,0:T(8,128)(2,1)S(1)} custom-call(s32[16,128]{1,0:T(8,128)S(1)} %get-tuple-element.56.refs_0_, bf16[128,32,128]{2,1,0:T(8,128)(2,1)S(1)} %get-tuple-element.58.refs_1_, bf16[512,512]{1,0:T(8,128)(2,1)} %get-tuple-element.59.refs_2_, bf16[512,128]{1,0:T(8,128)(2,1)} %get-tuple-element.60.refs_3_, ...), custom_call_target="tpu_custom_call" | custom-call | tf_op jit(solution)/shard_map/cond/branch_0_fun/exchange/pallas_call | solution.py:791
  149.0 1.0 copy.15
  (3 shorter events, 0.0 us)
